TPU v7x, 32 devices: a whole 2x2x4 slice. The times are simulated.
32 devices in a mesh: ens: 4 (over y, x), tile: 8 (over z, core).
Axes of the slice: x: 2, y: 2, z: 4, core: 2. Of those that a mesh axis runs over, the one named last changes fastest.
Arguments:
- air_latent_array: bfloat16 [4, 8, 16, 384], P('ens', 'tile'), may hold values from -6 to 6
- air_exchange_projection: bfloat16 [384, 128], replicated, may hold values from -0.3125 to 0.3125
- marine_latent_array: bfloat16 [4, 32, 64, 256], P('ens', None, 'tile'), may hold values from -6 to 6
- driver_projection_matrix: bfloat16 [128, 256], replicated, may hold values from -0.5 to 0.5
- spatial_kernel_taps: float32 [9, 256], replicated, may hold values from -1.5 to 1.5
- layernorm_multiplier: float32 [256], replicated, may hold values from 0.25 to 1.75
- pointwise_widen_matrix: bfloat16 [256, 1024], replicated, may hold values from -0.375 to 0.375
- pointwise_shrink_matrix: bfloat16 [1024, 256], replicated, may hold values from -0.1875 to 0.1875
- thermal_projection_matrix: bfloat16 [256, 128], replicated, may hold values from -0.375 to 0.375
- intersecting_air_sites: int32 [4, 32, 64], P(None, None, 'tile'), may hold values from 0 to 15, as said below
- margin_multiplier: int32 [4, 32, 64], P(None, None, 'tile'), may hold values from 1 to 8
- terrain_water_indicator: int32 [32, 64], P(None, 'tile'), may hold values from 0 to 1, as said below
- marine_successor_adjoint: bfloat16 [4, 32, 64, 256], P('ens', None, 'tile'), may hold values from -6 to 6
Outputs:
- marine_successor_latent: bfloat16 [4, 32, 64, 256], P('ens', None, 'tile')
- sst_atm: bfloat16 [4, 8, 16, 128], P('ens', 'tile')
- marine_latent_adjoint: bfloat16 [4, 32, 64, 256], P('ens', None, 'tile')
- grad_force: bfloat16 [128, 256], replicated
- grad_conv: bfloat16 [9, 256], replicated
- grad_gain: bfloat16 [256], replicated
- grad_up: bfloat16 [256, 1024], replicated
- grad_down: bfloat16 [1024, 256], replicated
Inputs may be any that keep to these rules, and one draw needn't show every extreme that they name: `intersecting_air_sites`: the index of an atmosphere cell that lies over the ocean cell's own tile: row * 2 + column, with the row among all 8 rows and the column among the 2 atmosphere columns over that tile. `terrain_water_indicator`: 1 marks a sea cell, 0 a land cell.
All inputs are finite; a program needn't handle non-finite values.
Results may differ from a plain program's by a relative error of at most 0.0082.
Values may be sent and summed in bfloat16 or wider, within the bound.
A program may use at most 64 MiB of HBM per device.

v0:
```python
import math

import jax
import jax.numpy as jnp
from jax import lax
from jax.sharding import PartitionSpec as P

SUBDIVISION = 4
KS = 3


def extended(cells, sides, width):
    for axis, dim in sides:
        count = lax.axis_size(axis)
        head = lax.slice_in_dim(cells, 0, width, axis=dim)
        tail = lax.slice_in_dim(cells, cells.shape[dim] - width, cells.shape[dim], axis=dim)
        cells = jnp.concatenate(
            [
                lax.ppermute(tail, axis, [(i, (i + 1) % count) for i in range(count)]),
                cells,
                lax.ppermute(head, axis, [((i + 1) % count, i) for i in range(count)]),
            ],
            axis=dim,
        )
    return cells


def layer_norm(values, gain):
    centred = values - jnp.mean(values, axis=-1, keepdims=True)
    spread = jnp.mean(centred * centred, axis=-1, keepdims=True)
    return centred * lax.rsqrt(spread + 1e-06) * gain


def regrid(flat_fluxes, cell_ids, margin):
    picked = jnp.take(flat_fluxes, cell_ids, axis=0).astype(jnp.float32)
    factor = margin.astype(jnp.float32)
    weighted = jnp.sum(factor[..., None] * picked, axis=0)
    return (weighted / jnp.sum(factor, axis=0)[..., None]).astype(jnp.bfloat16)


def marine_update_kernel(
    marine_present_latent,
    marine_driver_input,
    latent_adjoint,
    water_indicator_real,
    driver_projection_matrix,
    spatial_kernel_taps,
    layernorm_multiplier,
    pointwise_widen_matrix,
    pointwise_shrink_matrix,
    thermal_projection_matrix,
    haloed_latent,
    haloed_derivative,
):
    horizontal_sum_result, vertical_sum_result, feature_dimension = marine_present_latent.shape
    reach = KS // 2
    forcing_flat = marine_driver_input.reshape(-1, marine_driver_input.shape[-1])
    pushed = jnp.dot(
        forcing_flat, driver_projection_matrix, preferred_element_type=jnp.float32
    ).reshape(horizontal_sum_result, vertical_sum_result, feature_dimension)
    mixed = (marine_present_latent.astype(jnp.float32) + pushed).astype(jnp.bfloat16)
    padded = jnp.pad(haloed_latent(mixed), ((reach, reach), (0, 0), (0, 0))).astype(jnp.float32)
    conv_out = jnp.zeros(
        (horizontal_sum_result, vertical_sum_result, feature_dimension), jnp.float32
    )
    for row_off in range(KS):
        for col_off in range(KS):
            conv_out = (
                conv_out
                + spatial_kernel_taps[row_off * KS + col_off]
                * padded[
                    row_off : row_off + horizontal_sum_result,
                    col_off : col_off + vertical_sum_result,
                ]
            )
    normed_f, pull_norm = jax.vjp(
        layer_norm, conv_out.reshape(-1, feature_dimension), layernorm_multiplier
    )
    normed = normed_f.astype(jnp.bfloat16)
    hidden_pre = jnp.dot(normed, pointwise_widen_matrix, preferred_element_type=jnp.float32)
    hidden_f, pull_gelu = jax.vjp(jax.nn.gelu, hidden_pre)
    hidden = hidden_f.astype(jnp.bfloat16)
    mlp_out = jnp.dot(hidden, pointwise_shrink_matrix, preferred_element_type=jnp.float32)
    sea_column = water_indicator_real.reshape(-1, 1)
    marine_successor_latent = (
        sea_column * (mixed.reshape(-1, feature_dimension).astype(jnp.float32) + mlp_out)
    ).astype(jnp.bfloat16)
    thermal_highres_field = jnp.dot(
        marine_successor_latent, thermal_projection_matrix, preferred_element_type=jnp.float32
    )
    thermal_highres_field = thermal_highres_field.reshape(
        horizontal_sum_result // SUBDIVISION,
        SUBDIVISION,
        vertical_sum_result // SUBDIVISION,
        SUBDIVISION,
        thermal_highres_field.shape[-1],
    )
    marine_site_number = jnp.sum(
        water_indicator_real.reshape(
            horizontal_sum_result // SUBDIVISION,
            SUBDIVISION,
            vertical_sum_result // SUBDIVISION,
            SUBDIVISION,
        ),
        axis=(1, 3),
    )
    thermal_lowres_field = (
        jnp.sum(thermal_highres_field, axis=(1, 3))
        / jnp.maximum(marine_site_number, 1.0)[..., None]
    ).astype(jnp.bfloat16)
    masked_cot = (
        sea_column * latent_adjoint.reshape(-1, feature_dimension).astype(jnp.float32)
    ).astype(jnp.bfloat16)
    grad_down = jnp.dot(hidden.T, masked_cot, preferred_element_type=jnp.float32)
    hidden_cot = jnp.dot(masked_cot, pointwise_shrink_matrix.T, preferred_element_type=jnp.float32)
    pre_cot = pull_gelu(hidden_cot)[0].astype(jnp.bfloat16)
    grad_up = jnp.dot(normed.T, pre_cot, preferred_element_type=jnp.float32)
    normed_cot = jnp.dot(pre_cot, pointwise_widen_matrix.T, preferred_element_type=jnp.float32)
    conv_cot, grad_gain = pull_norm(normed_cot)
    conv_cot = conv_cot.reshape(horizontal_sum_result, vertical_sum_result, feature_dimension)
    tap_grads = []
    for row_off in range(KS):
        for col_off in range(KS):
            tap_grads.append(
                jnp.sum(
                    conv_cot
                    * padded[
                        row_off : row_off + horizontal_sum_result,
                        col_off : col_off + vertical_sum_result,
                    ],
                    axis=(0, 1),
                )
            )
    grad_padded = jnp.pad(haloed_derivative(conv_cot), ((reach, reach), (0, 0), (0, 0)))
    back = masked_cot.astype(jnp.float32).reshape(
        horizontal_sum_result, vertical_sum_result, feature_dimension
    )
    for row_off in range(KS):
        for col_off in range(KS):
            row_from = KS - 1 - row_off
            col_from = KS - 1 - col_off
            back = (
                back
                + spatial_kernel_taps[row_off * KS + col_off]
                * grad_padded[
                    row_from : row_from + horizontal_sum_result,
                    col_from : col_from + vertical_sum_result,
                ]
            )
    marine_latent_adjoint = back.astype(jnp.bfloat16)
    grad_force = jnp.dot(
        forcing_flat.T,
        marine_latent_adjoint.reshape(-1, feature_dimension),
        preferred_element_type=jnp.float32,
    )
    derivative_sequence = (grad_force, jnp.stack(tap_grads), grad_gain, grad_up, grad_down)
    return (
        marine_successor_latent.reshape(
            horizontal_sum_result, vertical_sum_result, feature_dimension
        ),
        thermal_lowres_field,
        marine_latent_adjoint,
        derivative_sequence,
    )


def pad_state_cols(values):
    return extended(values, (("tile", 1),), KS // 2)


def pad_grad_cols(values):
    return extended(values, (("tile", 1),), KS // 2)


def body(
    air_latent_array,
    air_exchange_projection,
    marine_latent_array,
    driver_projection_matrix,
    spatial_kernel_taps,
    layernorm_multiplier,
    pointwise_widen_matrix,
    pointwise_shrink_matrix,
    thermal_projection_matrix,
    intersecting_air_sites,
    margin_multiplier,
    terrain_water_indicator,
    marine_successor_adjoint,
):
    band = air_latent_array[0]
    band_rows, band_cols, atmos_width = band.shape
    fluxes = jnp.dot(
        band.reshape(-1, atmos_width), air_exchange_projection, preferred_element_type=jnp.float32
    ).astype(jnp.bfloat16)
    fluxes = fluxes.reshape(band_rows, band_cols, fluxes.shape[-1])
    strip = lax.all_to_all(fluxes, "tile", split_axis=1, concat_axis=0, tiled=True)
    marine_driver_input = regrid(
        strip.reshape(-1, strip.shape[-1]), intersecting_air_sites, margin_multiplier
    )
    water_indicator_real = terrain_water_indicator.astype(jnp.float32)
    marine_successor_latent, thermal_lowres_field, marine_latent_adjoint, derivative_sequence = (
        marine_update_kernel(
            marine_latent_array[0],
            marine_driver_input,
            marine_successor_adjoint[0],
            water_indicator_real,
            driver_projection_matrix,
            spatial_kernel_taps,
            layernorm_multiplier,
            pointwise_widen_matrix,
            pointwise_shrink_matrix,
            thermal_projection_matrix,
            pad_state_cols,
            pad_grad_cols,
        )
    )
    thermal_strip_slice = lax.all_to_all(
        thermal_lowres_field, "tile", split_axis=0, concat_axis=1, tiled=True
    )
    cell_total = (
        lax.axis_size("ens")
        * lax.axis_size("tile")
        * marine_successor_latent.shape[0]
        * marine_successor_latent.shape[1]
    )
    grad_scale = 1.0 / math.sqrt(cell_total)
    grad_force, grad_conv, grad_gain, grad_up, grad_down = derivative_sequence
    accumulated_result = lax.psum(
        (grad_force, grad_conv, grad_gain, grad_up, grad_down), ("ens", "tile")
    )
    scaled = [(values * grad_scale).astype(jnp.bfloat16) for values in accumulated_result]
    return (
        marine_successor_latent[None],
        thermal_strip_slice[None],
        marine_latent_adjoint[None],
        scaled[0],
        scaled[1],
        scaled[2],
        scaled[3],
        scaled[4],
    )


def solution(mesh):
    return jax.shard_map(
        body,
        mesh=mesh,
        in_specs=(
            P("ens", "tile", None, None),
            P(),
            P("ens", None, "tile", None),
            P(),
            P(),
            P(),
            P(),
            P(),
            P(),
            P(None, None, "tile"),
            P(None, None, "tile"),
            P(None, "tile"),
            P("ens", None, "tile", None),
        ),
        out_specs=(
            P("ens", None, "tile", None),
            P("ens", "tile", None, None),
            P("ens", None, "tile", None),
            P(),
            P(),
            P(),
            P(),
            P(),
        ),
        check_vma=False,
    )
```

profile of v0, /device:TPU:0, one launch (start us, length us, event | category | flops | bytes accessed | tf_op | source)
XLA Modules:
  0.0 193.2 jit_solution(1567825441437145377)
XLA Ops:
  7.2 1.1 fusion.3
  8.3 0.6 copy.62
  8.9 6.4 %all-to-all-start = ((bf16[8,2,128]{2,1,0:T(2,128)(2,1)}), bf16[8,2,128]{2,1,0:T(2,128)(2,1)S(1)}, u32[]{:S(2)}, u32[]{:S(2)}) async-start(bf16[8,2,128]{2,1,0:T(2,128)(2,1)} %bitcast.92), calls=%async_computation | async-start | bytes 8192 | tf_op jit(solution)/shard_map/all_to_all | solution.py:196
  15.3 0.7 copy-done.9
  16.2 0.6 copy-done.7
  16.9 0.7 copy-done.10
  18.0 2.8 %all-to-all-done = bf16[8,2,128]{2,1,0:T(2,128)(2,1)S(1)} async-done(((bf16[8,2,128]{2,1,0:T(2,128)(2,1)}), bf16[8,2,128]{2,1,0:T(2,128)(2,1)S(1)}, u32[]{:S(2)}, u32[]{:S(2)}) %all-to-all-start) | async-done | bytes 4128 | tf_op jit(solution)/shard_map/all_to_all | solution.py:196
  20.8 3.2 %gather_fusion = bf16[1024,128]{1,0:T(8,128)(2,1)S(1)} fusion(bf16[16,128]{1,0:T(8,128)(2,1)S(1)} %bitcast.93, s32[1024]{0:T(1024)S(1)} %broadcast_clamp_fusion), kind=kCustom, calls=%fused_computation | custom fusion | bytes 528384 | tf_op jit(solution)/shard_map/jit(_take)/gather | solution.py:35
  25.3 3.5 %collective-permute-start.1 = (bf16[32,1,256]{2,1,0:T(2,128)(2,1)S(1)}, bf16[32,1,256]{2,1,0:T(2,128)(2,1)S(1)}, u32[]{:S(2)}, u32[]{:S(2)}) collective-permute-start(bf16[32,1,256]{2,1,0:T(2,128)(2,1)S(1)} %get-tuple-element.32), channel_id=1, source_target_pairs={{1,0},{2,1},{3,2},{4,3},{5,4},{6,5},{7,6},{0,7},{9,8},{10,9},{11,1... | collective-permute-start | bytes 49160 | tf_op jit(solution)/shard_map/ppermute | solution.py:21
  29.0 1.3 collective-permute-done
  31.2 0.7 copy-done.8
  32.8 1.6 fusion.31
  34.4 0.9 fusion.10
  36.3 3.6 %collective-permute-start.3 = (f32[32,1,256]{2,1,0:T(1,128)S(1)}, f32[32,1,256]{2,1,0:T(1,128)S(1)}, u32[]{:S(2)}, u32[]{:S(2)}) collective-permute-start(f32[32,1,256]{2,1,0:T(1,128)S(1)} %get-tuple-element.30), channel_id=1, source_target_pairs={{1,0},{2,1},{3,2},{4,3},{5,4},{6,5},{7,6},{0,7},{9,8},{10,9},{11,1... | collective-permute-start | bytes 98312 | tf_op jit(solution)/shard_map/ppermute | solution.py:21
  39.9 1.4 fusion.38
  42.0 0.9 convolution_bitcast_fusion
  44.5 0.7 divide_convert_fusion.1
  45.2 4.8 %all-to-all-start.1 = ((bf16[8,2,128]{2,1,0:T(2,128)(2,1)}), bf16[8,2,128]{2,1,0:T(2,128)(2,1)S(1)}, u32[]{:S(2)}, u32[]{:S(2)}) async-start(bf16[8,2,128]{2,1,0:T(2,128)(2,1)} %divide_convert_fusion.1), calls=%async_computation.1 | async-start | bytes 8192 | tf_op jit(solution)/shard_map/all_to_all | solution.py:217
  50.1 41.1 %all-reduce.2 = (f32[9,256]{1,0:T(8,128)S(1)}, f32[256]{0:T(256)S(1)}) all-reduce(f32[9,256]{1,0:T(8,128)S(1)} %stack.39, f32[256]{0:T(256)S(1)} %get-tuple-element.17), channel_id=1, replica_groups=mesh['ens'=4,'tile'=8] {'ens','tile'}, use_global_device_ids=true, to_apply=%region_18.19 | all-reduce | flops 2560 | bytes 20480 | tf_op jit(solution)/shard_map/psum | solution.py:228
  91.2 0.6 multiply_convert_fusion.5
  92.3 88.8 %all-reduce.6.cloned.1.call-done = (f32[128,256]{1,0:T(8,128)}, f32[256,1024]{1,0:T(8,128)}, f32[1024,256]{1,0:T(8,128)}) async-done(((f32[128,256]{1,0:T(8,128)}, f32[256,1024]{1,0:T(8,128)}, f32[1024,256]{1,0:T(8,128)}), (f32[128,256]{1,0:T(8,128)}, f32[256,1024]{1,0:T(8,128)}, f32[1024,256]{1,0:T(8,128)})) %all-reduce.6.cloned.1.call-update) | async-done | bytes 2228240 | tf_op jit(solution)/shard_map/psum | solution.py:228
  181.1 1.6 multiply_convert_fusion.4
  182.7 2.1 %multiply_convert_fusion.1 = bf16[256,1024]{1,0:T(8,128)(2,1)} fusion(f32[256,1024]{1,0:T(8,128)} %get-tuple-element.22), kind=kLoop, calls=%fused_computation.19 | loop fusion | flops 524288 | bytes 1572864 | tf_op jit(solution)/shard_map/convert_element_type | solution.py:231
  184.8 0.9 multiply_convert_fusion
  (79 shorter events, 8.3 us)
Async XLA Ops:
  7.2 24.0 %copy-start = (bf16[256,1024]{1,0:T(8,128)(2,1)S(1)}, bf16[256,1024]{1,0:T(8,128)(2,1)}, u32[]{:S(2)}) copy-start(bf16[256,1024]{1,0:T(8,128)(2,1)} %param.19) | copy-start | bytes 1572868
  8.3 7.0 %copy-start.6 = (s32[4,32,8]{1,2,0:T(8,128)S(1)}, s32[4,32,8]{1,2,0:T(8,128)}, u32[]{:S(2)}) copy-start(s32[4,32,8]{1,2,0:T(8,128)} %param.22) | copy-start | bytes 12292
  8.9 11.9 %all-to-all-start = ((bf16[8,2,128]{2,1,0:T(2,128)(2,1)}), bf16[8,2,128]{2,1,0:T(2,128)(2,1)S(1)}, u32[]{:S(2)}, u32[]{:S(2)}) async-start(bf16[8,2,128]{2,1,0:T(2,128)(2,1)} %bitcast.92), calls=%async_computation | async-start | bytes 8192 | tf_op jit(solution)/shard_map/all_to_all | solution.py:196
  15.2 165.8 %all-reduce.6.cloned.1.call-start = ((), (), s32[]{:S(2)}) async-start(), calls=%async_computation.2 | async-start | bytes 4456448 | tf_op jit(solution)/shard_map/psum | solution.py:228
  15.3 0.7 copy-start.9
  16.1 0.7 copy-start.7
  16.9 0.7 copy-start.10
  24.0 0.9 copy-start.12
  24.0 0.9 copy-start.13
  25.2 5.2 %collective-permute-start = (bf16[32,1,256]{2,1,0:T(2,128)(2,1)S(1)}, bf16[32,1,256]{2,1,0:T(2,128)(2,1)S(1)}, u32[]{:S(2)}, u32[]{:S(2)}) collective-permute-start(bf16[32,1,256]{2,1,0:T(2,128)(2,1)S(1)} %get-tuple-element.31), channel_id=1, source_target_pairs={{0,1},{1,2},{2,3},{3,4},{4,5},{5,6},{6,7},{7,0},{8,9},{9,10},{10,1... | collective-permute-start | bytes 49160 | tf_op jit(solution)/shard_map/ppermute | solution.py:19
  25.3 5.1 %collective-permute-start.1 = (bf16[32,1,256]{2,1,0:T(2,128)(2,1)S(1)}, bf16[32,1,256]{2,1,0:T(2,128)(2,1)S(1)}, u32[]{:S(2)}, u32[]{:S(2)}) collective-permute-start(bf16[32,1,256]{2,1,0:T(2,128)(2,1)S(1)} %get-tuple-element.32), channel_id=1, source_target_pairs={{1,0},{2,1},{3,2},{4,3},{5,4},{6,5},{7,6},{0,7},{9,8},{10,9},{11,1... | collective-permute-start | bytes 49160 | tf_op jit(solution)/shard_map/ppermute | solution.py:21
  31.2 0.7 copy-start.8
  31.9 0.9 copy-start.3
  32.8 1.6 copy-start.11
  36.3 5.2 %collective-permute-start.2 = (f32[32,1,256]{2,1,0:T(1,128)S(1)}, f32[32,1,256]{2,1,0:T(1,128)S(1)}, u32[]{:S(2)}, u32[]{:S(2)}) collective-permute-start(f32[32,1,256]{2,1,0:T(1,128)S(1)} %get-tuple-element.29), channel_id=1, source_target_pairs={{0,1},{1,2},{2,3},{3,4},{4,5},{5,6},{6,7},{7,0},{8,9},{9,10},{10,1... | collective-permute-start | bytes 98312 | tf_op jit(solution)/shard_map/ppermute | solution.py:19
  36.3 5.2 %collective-permute-start.3 = (f32[32,1,256]{2,1,0:T(1,128)S(1)}, f32[32,1,256]{2,1,0:T(1,128)S(1)}, u32[]{:S(2)}, u32[]{:S(2)}) collective-permute-start(f32[32,1,256]{2,1,0:T(1,128)S(1)} %get-tuple-element.30), channel_id=1, source_target_pairs={{1,0},{2,1},{3,2},{4,3},{5,4},{6,5},{7,6},{0,7},{9,8},{10,9},{11,1... | collective-permute-start | bytes 98312 | tf_op jit(solution)/shard_map/ppermute | solution.py:21
  42.0 1.0 copy-start.4
  43.0 0.8 copy-start.5
  43.8 0.7 copy-start.2
  45.2 47.1 %all-to-all-start.1 = ((bf16[8,2,128]{2,1,0:T(2,128)(2,1)}), bf16[8,2,128]{2,1,0:T(2,128)(2,1)S(1)}, u32[]{:S(2)}, u32[]{:S(2)}) async-start(bf16[8,2,128]{2,1,0:T(2,128)(2,1)} %divide_convert_fusion.1), calls=%async_computation.1 | async-start | bytes 8192 | tf_op jit(solution)/shard_map/all_to_all | solution.py:217
  181.1 3.8 %copy-start.1 = (f32[1024,256]{1,0:T(8,128)S(1)}, f32[1024,256]{1,0:T(8,128)}, u32[]{:S(2)}) copy-start(f32[1024,256]{1,0:T(8,128)} %get-tuple-element.23) | copy-start | bytes 3145732
Sparse Core Ops, SparseCore 0:
  43.1 137.9 all-reduce.5
where the time goes:
time: 194 us; the launch traced here: 193 us
  waiting for transfers between devices  93.1 us (48%)
  blocking collectives  41.1 us (21%)
  starting transfers between devices  18.4 us (9%)
  between operations  14.3 us (7%)
  local copies, waits for them, and re-layouts  10.1 us (5%)
  other arithmetic  8.55 us (4%)
  matrix products  7.59 us (4%)
    psum x1, waiting for transfers between devices, body(): lax.psum((grad_force, grad_conv, grad_gain, grad_up, grad_down), ('ens',...  88.8 us
    psum x1, blocking collectives, body(): lax.psum((grad_force, grad_conv, grad_gain, grad_up, grad_down), ('ens',...  41.1 us
    ppermute x2, starting transfers between devices, extended(): lax.ppermute(head, axis, [((i + 1) % count, i) for i in range(count)])  7.12 us
    all_to_all x1, starting transfers between devices, body(): lax.all_to_all(fluxes, 'tile', split_axis=1, concat_axis=0, tiled=True)  6.35 us
    unnamed x32, local copies, waits for them, and re-layouts  5.81 us
    convert_element_type x5, other arithmetic, body(): (values * grad_scale).astype(jnp.bfloat16)  5.76 us
    all_to_all x1, starting transfers between devices, body(): lax.all_to_all(thermal_lowres_field, 'tile', split_axis=0, concat_axis=1,...  4.82 us
  transfers between devices with their start and end apart: 7, of which 5 were waited for; matrix products, arithmetic and copies ran while one was open for 2% of the time, Pallas kernels for 0%

commit v1 on v0

--- a/solution.py
+++ b/solution.py
@@ -1,12 +1,270 @@
+import functools
 import math
 
 import jax
 import jax.numpy as jnp
 from jax import lax
+from jax.experimental import pallas as pl
+from jax.experimental.pallas import tpu as pltpu
 from jax.sharding import PartitionSpec as P
 
 SUBDIVISION = 4
 KS = 3
+LANES = 128
+SLAB = 8
+MESH = pl.DeviceIdType.MESH
+
+
+def pack_plan(shapes):
+    plan, at = [], 0
+    for which, (rows, cols) in enumerate(shapes):
+        for col in range(0, cols, LANES):
+            plan.append((which, col, at, rows))
+            at += rows
+    return plan, at
+
+
+def reduce_kernel(
+    scale,
+    ne,
+    nt,
+    rows,
+    plan,
+    used,
+    up_ref,
+    down_ref,
+    force_ref,
+    small_ref,
+    therm_ref,
+    up_out,
+    down_out,
+    force_out,
+    small_out,
+    therm_out,
+    packed,
+    from_core,
+    halves,
+    from_ens,
+    part,
+    from_z,
+    whole,
+    therm_in,
+    t_send,
+    t_recv,
+    a_send,
+    a_recv,
+    b_send,
+    b_recv,
+    c_send,
+    c_recv,
+    d_send,
+    d_recv,
+    e_send,
+    e_recv,
+    f_send,
+    f_recv,
+):
+    nz = nt // 2
+    block = nz * rows
+    half = ne * block
+    ens = lax.axis_index("ens")
+    tile = lax.axis_index("tile")
+    z = tile // 2
+    core = tile % 2
+    other = 1 - core
+    mate = {"tile": z * 2 + other}
+
+    def send(src, dst, s_sem, r_sem, device):
+        copy = pltpu.make_async_remote_copy(
+            src_ref=src,
+            dst_ref=dst,
+            send_sem=s_sem,
+            recv_sem=r_sem,
+            device_id=device,
+            device_id_type=MESH,
+        )
+        copy.start()
+        return copy
+
+    barrier = pltpu.get_barrier_semaphore()
+    for o in range(1, nt):
+        pl.semaphore_signal(
+            barrier, inc=1, device_id={"tile": (tile + o) % nt}, device_id_type=MESH
+        )
+    for o in range(1, ne):
+        pl.semaphore_signal(
+            barrier, inc=1, device_id={"ens": (ens + o) % ne}, device_id_type=MESH
+        )
+
+    ins = (up_ref, down_ref, force_ref, small_ref)
+    for which, col, at, count in plan:
+        packed[at : at + count, :] = ins[which][:, col : col + LANES].astype(jnp.bfloat16)
+    if used < 2 * half:
+        packed[used : 2 * half, :] = jnp.zeros((2 * half - used, LANES), jnp.bfloat16)
+    pl.semaphore_wait(barrier, nt - 1 + ne - 1)
+
+    def at_block(h, e):
+        return pl.ds(pl.multiple_of((h * ne + e) * block, 16), block)
+
+    order = list(range(1, ne)) + [0]
+    a_copies = []
+    for o in order:
+        e = (ens + o) % ne
+        a_copies.append(
+            send(
+                packed.at[at_block(other, e)],
+                from_core.at[o],
+                a_send.at[o],
+                a_recv.at[o],
+                mate,
+            )
+        )
+    t_copies = []
+    for o in range(1, nt):
+        to = (tile + o) % nt
+        t_copies.append(
+            send(
+                therm_ref.at[to],
+                therm_in.at[o],
+                t_send.at[o],
+                t_recv.at[o],
+                {"tile": to},
+            )
+        )
+    b_copies = []
+    for o, copy in zip(order, a_copies):
+        e = (ens + o) % ne
+        copy.wait_recv()
+        halves[o] = (
+            packed[at_block(core, e), :].astype(jnp.float32) + from_core[o].astype(jnp.float32)
+        ).astype(jnp.bfloat16)
+        if o:
+            b_copies.append(
+                send(halves.at[o], from_ens.at[o], b_send.at[o], b_recv.at[o], {"ens": e})
+            )
+    total = halves[0].astype(jnp.float32)
+    for o, copy in zip(range(1, ne), b_copies):
+        copy.wait_recv()
+        total = total + from_ens[o].astype(jnp.float32)
+    part[...] = total.astype(jnp.bfloat16)
+
+    def at_chunk(where):
+        return pl.ds(pl.multiple_of(where * rows, 16), rows)
+
+    c_copies = []
+    for o in range(1, nz):
+        to = (z + o) % nz
+        c_copies.append(
+            send(
+                part.at[at_chunk(to)],
+                from_z.at[o],
+                c_send.at[o],
+                c_recv.at[o],
+                {"tile": to * 2 + core},
+            )
+        )
+    mine = part[at_chunk(z), :].astype(jnp.float32)
+    for o, copy in zip(range(1, nz), c_copies):
+        copy.wait_recv()
+        mine = mine + from_z[o].astype(jnp.float32)
+    spot = (core * ne + ens) * nz + z
+    whole[at_chunk(spot), :] = (mine * scale).astype(jnp.bfloat16)
+    d_copies = []
+    for o in range(1, nz):
+        to = (z + o) % nz
+        d_copies.append(
+            send(
+                whole.at[at_chunk(spot)],
+                whole.at[at_chunk(spot)],
+                d_send.at[o],
+                d_recv.at[o],
+                {"tile": to * 2 + core},
+            )
+        )
+    for copy in d_copies:
+        copy.wait_recv()
+    e_copies = []
+    for o in range(1, ne):
+        e_copies.append(
+            send(
+                whole.at[at_block(core, ens)],
+                whole.at[at_block(core, ens)],
+                e_send.at[o],
+                e_recv.at[o],
+                {"ens": (ens + o) % ne},
+            )
+        )
+    f_copies = [
+        send(
+            whole.at[at_block(core, ens)],
+            whole.at[at_block(core, ens)],
+            f_send.at[0],
+            f_recv.at[0],
+            mate,
+        )
+    ]
+    for o, copy in zip(range(1, ne), e_copies):
+        copy.wait_recv()
+        e = (ens + ne - o) % ne
+        f_copies.append(
+            send(
+                whole.at[at_block(core, e)],
+                whole.at[at_block(core, e)],
+                f_send.at[o],
+                f_recv.at[o],
+                mate,
+            )
+        )
+    therm_out[tile] = therm_ref[tile]
+    for o, copy in zip(range(1, nt), t_copies):
+        copy.wait_recv()
+        therm_out[(tile + nt - o) % nt] = therm_in[o]
+    for copy in f_copies:
+        copy.wait_recv()
+    for copy in a_copies + t_copies + b_copies + c_copies + d_copies + e_copies + f_copies:
+        copy.wait_send()
+    outs = (up_out, down_out, force_out, small_out)
+    for which, col, at, count in plan:
+        outs[which][:, col : col + LANES] = whole[at : at + count, :]
+
+
+def reduce_gradients(up, down, force, small, therm, scale):
+    ne, nt = lax.axis_size("ens"), lax.axis_size("tile")
+    nz = nt // 2
+    plan, used = pack_plan([up.shape, down.shape, force.shape, small.shape])
+    rows = -(-used // (2 * ne * nz * 16)) * 16
+    block = nz * rows
+    bf16 = jnp.bfloat16
+    dma = pltpu.SemaphoreType.DMA
+    vmem = pl.BlockSpec(memory_space=pltpu.VMEM)
+    return pl.pallas_call(
+        functools.partial(reduce_kernel, scale, ne, nt, rows, plan, used),
+        out_shape=[
+            jax.ShapeDtypeStruct(up.shape, bf16),
+            jax.ShapeDtypeStruct(down.shape, bf16),
+            jax.ShapeDtypeStruct(force.shape, bf16),
+            jax.ShapeDtypeStruct(small.shape, bf16),
+            jax.ShapeDtypeStruct(therm.shape, therm.dtype),
+        ],
+        in_specs=[vmem] * 5,
+        out_specs=[vmem] * 5,
+        scratch_shapes=[
+            pltpu.VMEM((2 * ne * block, LANES), bf16),
+            pltpu.VMEM((ne, block, LANES), bf16),
+            pltpu.VMEM((ne, block, LANES), bf16),
+            pltpu.VMEM((ne, block, LANES), bf16),
+            pltpu.VMEM((block, LANES), bf16),
+            pltpu.VMEM((nz, rows, LANES), bf16),
+            pltpu.VMEM((2 * ne * block, LANES), bf16),
+            pltpu.VMEM(therm.shape, therm.dtype),
+        ]
+        + [dma((nt,)), dma((nt,))]
+        + [dma((ne,)), dma((ne,))] * 2
+        + [dma((nz,)), dma((nz,))] * 2
+        + [dma((ne,)), dma((ne,))] * 2,
+        compiler_params=pltpu.CompilerParams(collective_id=1, has_side_effects=True),
+        name="reduce_gradients",
+    )(up, down, force, small, therm)
 
 
 def extended(cells, sides, width):
@@ -214,9 +472,6 @@
             pad_grad_cols,
         )
     )
-    thermal_strip_slice = lax.all_to_all(
-        thermal_lowres_field, "tile", split_axis=0, concat_axis=1, tiled=True
-    )
     cell_total = (
         lax.axis_size("ens")
         * lax.axis_size("tile")
@@ -225,19 +480,30 @@
     )
     grad_scale = 1.0 / math.sqrt(cell_total)
     grad_force, grad_conv, grad_gain, grad_up, grad_down = derivative_sequence
-    accumulated_result = lax.psum(
-        (grad_force, grad_conv, grad_gain, grad_up, grad_down), ("ens", "tile")
-    )
-    scaled = [(values * grad_scale).astype(jnp.bfloat16) for values in accumulated_result]
+    taps, features = grad_conv.shape
+    small = jnp.pad(
+        jnp.concatenate([grad_conv, grad_gain.reshape(1, features)]),
+        ((0, -(taps + 1) % 16), (0, 0)),
+    )
+    tiles, columns, quantity = thermal_lowres_field.shape
+    therm = jnp.pad(
+        thermal_lowres_field.astype(jnp.float32), ((0, 0), (0, SLAB - columns), (0, 0))
+    )
+    up, down, force, small, therm = reduce_gradients(
+        grad_up, grad_down, grad_force, small, therm, grad_scale
+    )
+    thermal_strip_slice = (
+        therm[:, :columns].reshape(1, tiles * columns, quantity).astype(jnp.bfloat16)
+    )
     return (
         marine_successor_latent[None],
         thermal_strip_slice[None],
         marine_latent_adjoint[None],
-        scaled[0],
-        scaled[1],
-        scaled[2],
-        scaled[3],
-        scaled[4],
+        force,
+        small[:taps],
+        small[taps],
+        up,
+        down,
     )
 
 

time: 194 us -> 80.1 us (0.41)
  waiting for transfers between devices: 93.1 us -> 4.86 us
  blocking collectives: 41.1 us -> 0 us
  Pallas kernels: 0 us -> 33.6 us
  between operations: 14.3 us -> 0.93 us
  local copies, waits for them, and re-layouts: 10.1 us -> 16.2 us
  other arithmetic: 8.55 us -> 2.81 us
  starting transfers between devices: 18.4 us -> 13.6 us
    psum x1 -> x0, waiting for transfers between devices: 88.8 us -> none  [body(): lax.psum((grad_force, grad_conv, grad_gain, grad_up, grad_down), ('ens',...]
    psum x1 -> x0, blocking collectives: 41.1 us -> none  [body(): lax.psum((grad_force, grad_conv, grad_gain, grad_up, grad_down), ('ens',...]
    pallas_call x0 -> x1, Pallas kernels: none -> 33.6 us  [reduce_gradients(): pl.pallas_call(functools.partial(reduce_kernel, scale, ne, nt, rows, plan...]
    convert_element_type x5 -> x0, other arithmetic: 5.76 us -> none  [body(): (values * grad_scale).astype(jnp.bfloat16)]
    all_to_all x1 -> x0, starting transfers between devices: 4.82 us -> none  [body(): lax.all_to_all(thermal_lowres_field, 'tile', split_axis=0, concat_axis=1,...]
    unnamed x32 -> x37, local copies, waits for them, and re-layouts: 5.81 us -> 8.72 us
    slice x0 -> x2, local copies, waits for them, and re-layouts: none -> 2.56 us  [the longest x1 1.35 us: body(): therm[:, :columns].reshape(1, tiles * columns, quantity)]
  transfers between devices with their start and end apart: 7 -> 5, of which waited for: 5 -> 2; matrix products, arithmetic and copies ran while one was open for 2% -> 3% of each run, Pallas kernels for 0% -> 0%
where the time goes in v1:
time: 80.1 us; the launch traced here: 79.6 us
  Pallas kernels  33.6 us (42%)
  local copies, waits for them, and re-layouts  16.2 us (20%)
  starting transfers between devices  13.6 us (17%)
  matrix products  7.63 us (10%)
  waiting for transfers between devices  4.86 us (6%)
  other arithmetic  2.81 us (4%)
  between operations  0.93 us (1%)
    pallas_call x1, Pallas kernels, reduce_gradients(): pl.pallas_call(functools.partial(reduce_kernel, scale, ne, nt, rows, plan...  33.6 us
    unnamed x37, local copies, waits for them, and re-layouts  8.72 us
    ppermute x2, starting transfers between devices, extended(): lax.ppermute(head, axis, [((i + 1) % count, i) for i in range(count)])  7.13 us
    all_to_all x1, starting transfers between devices, body(): lax.all_to_all(fluxes, 'tile', split_axis=1, concat_axis=0, tiled=True)  6.35 us
    all_to_all x1, waiting for transfers between devices, body(): lax.all_to_all(fluxes, 'tile', split_axis=1, concat_axis=0, tiled=True)  3.51 us
    gather x1, local copies, waits for them, and re-layouts, regrid(): picked = jnp.take(flat_fluxes, cell_ids, axis=0).astype(jnp.float32)  3.2 us
    dot_general x1, matrix products, marine_update_kernel(): jnp.dot(hidden.T, masked_cot, preferred_element_type=jnp.float32)  1.64 us
  transfers between devices with their start and end apart: 5, of which 2 were waited for; matrix products, arithmetic and copies ran while one was open for 3% of the time, Pallas kernels for 0%

profile of v1, /device:TPU:0, one launch (start us, length us, event | category | flops | bytes accessed | tf_op | source)
XLA Modules:
  0.0 79.6 jit_solution(2900156202858158264)
XLA Ops:
  0.6 1.1 %fusion.3 = bf16[1,16,128]{2,1,0:T(8,128)(2,1)S(1)} fusion(bf16[384,128]{1,0:T(8,128)(2,1)} %param.14, bf16[1,1,16,384]{3,2,1,0:T(8,128)(2,1)} %param.13), kind=kOutput, calls=%fused_computation.10 | convolution fusion | flops 1574912 | bytes 114688 | tf_op jit(solution)/shard_map/dot_general | solution.py:450
  1.8 0.6 copy.62
  2.4 6.4 %all-to-all-start = ((bf16[8,2,128]{2,1,0:T(2,128)(2,1)}), bf16[8,2,128]{2,1,0:T(2,128)(2,1)S(1)}, u32[]{:S(2)}, u32[]{:S(2)}) async-start(bf16[8,2,128]{2,1,0:T(2,128)(2,1)} %bitcast.94), calls=%async_computation | async-start | bytes 8192 | tf_op jit(solution)/shard_map/all_to_all | solution.py:454
  9.0 0.6 copy-done.10
  9.9 0.6 copy-done.11
  10.7 3.5 %all-to-all-done = bf16[8,2,128]{2,1,0:T(2,128)(2,1)S(1)} async-done(((bf16[8,2,128]{2,1,0:T(2,128)(2,1)}), bf16[8,2,128]{2,1,0:T(2,128)(2,1)S(1)}, u32[]{:S(2)}, u32[]{:S(2)}) %all-to-all-start) | async-done | bytes 4128 | tf_op jit(solution)/shard_map/all_to_all | solution.py:454
  14.2 3.2 %gather_fusion = bf16[1024,128]{1,0:T(8,128)(2,1)S(1)} fusion(bf16[16,128]{1,0:T(8,128)(2,1)S(1)} %bitcast.95, s32[1024]{0:T(1024)S(1)} %broadcast_clamp_fusion), kind=kCustom, calls=%fused_computation | custom fusion | bytes 528384 | tf_op jit(solution)/shard_map/jit(_take)/gather | solution.py:293
  18.7 3.5 %collective-permute-start.1 = (bf16[32,1,256]{2,1,0:T(2,128)(2,1)S(1)}, bf16[32,1,256]{2,1,0:T(2,128)(2,1)S(1)}, u32[]{:S(2)}, u32[]{:S(2)}) collective-permute-start(bf16[32,1,256]{2,1,0:T(2,128)(2,1)S(1)} %get-tuple-element.37), channel_id=1, source_target_pairs={{1,0},{2,1},{3,2},{4,3},{5,4},{6,5},{7,6},{0,7},{9,8},{10,9},{11,1... | collective-permute-start | bytes 49160 | tf_op jit(solution)/shard_map/ppermute | solution.py:279
  22.5 1.3 %collective-permute-done = bf16[32,1,256]{2,1,0:T(2,128)(2,1)S(1)} collective-permute-done((bf16[32,1,256]{2,1,0:T(2,128)(2,1)S(1)}, bf16[32,1,256]{2,1,0:T(2,128)(2,1)S(1)}, u32[]{:S(2)}, u32[]{:S(2)}) %collective-permute-start) | collective-permute-done | bytes 16416 | tf_op jit(solution)/shard_map/ppermute | solution.py:277
  24.7 0.7 copy-done.8
  26.4 0.9 %fusion.10 = bf16[256,1024]{1,0:T(8,128)(2,1)S(1)} fusion(f32[256,1024]{1,0:T(8,128)S(1)} %fusion.39, bf16[1024,256]{1,0:T(8,128)(2,1)S(1)} %copy-done.12, bf16[1,32,8,256]{3,2,1,0:T(8,128)(2,1)S(1)} %copy-done.3, f32[256]{0:T(256)S(1)} %mul.301), kind=kOutput, calls=%fused_computation.17 | convolution fusion | flops 139657216 | bytes 2229248 | tf_op jit(solution)/shard_map/dot_general | solution.py:373
  27.7 1.4 %fusion.38.up_ref = f32[256,1024]{1,0:T(8,128)} fusion(bf16[256,1024]{1,0:T(8,128)(2,1)S(1)} %fusion.10, f32[32,8,256]{2,1,0:T(8,128)S(1)} %get-tuple-element.33, f32[256]{0:T(256)S(1)} %copy-done.8, f32[256]{0:T(256)S(1)} %rsqrt.10, f32[256]{0:T(256)S(1)} %div.41), kind=kOutput, calls=%fused_computation.91 | convolution fusion | flops 134479872 | bytes 1838080 | tf_op jit(solution)/shard_map/dot_general | solution.py:375
  29.2 1.6 %fusion.31.down_ref = f32[1024,256]{1,0:T(8,128)} fusion(bf16[1,32,8,256]{3,2,1,0:T(8,128)(2,1)S(1)} %copy-done.3, f32[256]{0:T(256)S(1)} %mul.301, f32[256,1024]{1,0:T(8,128)S(1)} %fusion.39), kind=kOutput, calls=%fused_computation.74 | convolution fusion | flops 136773632 | bytes 2229248 | tf_op jit(solution)/shard_map/dot_general | solution.py:372
  32.0 3.6 %collective-permute-start.3 = (f32[32,1,256]{2,1,0:T(1,128)S(1)}, f32[32,1,256]{2,1,0:T(1,128)S(1)}, u32[]{:S(2)}, u32[]{:S(2)}) collective-permute-start(f32[32,1,256]{2,1,0:T(1,128)S(1)} %get-tuple-element.35), channel_id=1, source_target_pairs={{1,0},{2,1},{3,2},{4,3},{5,4},{6,5},{7,6},{0,7},{9,8},{10,9},{11,1... | collective-permute-start | bytes 98312 | tf_op jit(solution)/shard_map/ppermute | solution.py:279
  35.9 0.6 pad_convert_fusion.therm_ref
  36.6 0.6 pad.20.small_ref
  37.7 1.0 %convolution_bitcast_fusion.force_ref = f32[128,256]{1,0:T(8,128)} fusion(bf16[32,8,256]{2,1,0:T(8,128)(2,1)S(1)} %fusion.19, f32[32,8,128]{2,1,0:T(8,128)S(1)} %multiply_reduce_fusion, f32[32,8]{1,0:T(8,128)S(1)} %copy.54), kind=kOutput, calls=%fused_computation.8 | convolution fusion | flops 16842752 | bytes 394240 | tf_op jit(solution)/shard_map/dot_general | solution.py:409
  38.6 33.6 %reduce_gradients.1 = (bf16[256,1024]{1,0:T(8,128)(2,1)}, bf16[1024,256]{1,0:T(8,128)(2,1)}, bf16[128,256]{1,0:T(8,128)(2,1)}, bf16[16,256]{1,0:T(8,128)(2,1)}, f32[8,8,128]{2,1,0:T(8,128)}) custom-call(f32[256,1024]{1,0:T(8,128)} %fusion.38.up_ref, f32[1024,256]{1,0:T(8,128)} %fusion.31.down_ref, f32[128,256]{1,0:T(8,128)} %convolution_bitcast_fusion.force_ref, ...), custom_call_target="tpu_custom_call" | custom-call | tf_op jit(solution)/shard_map/reduce_gradients/pallas_call | solution.py:240
  72.2 1.2 %slice_reduce_fusion = bf16[256]{0:T(256)(128)(2,1)} fusion(bf16[16,256]{1,0:T(8,128)(2,1)} %get-tuple-element.15), kind=kLoop, calls=%fused_computation.86 | loop fusion | bytes 1024 | tf_op jit(solution)/shard_map/slice | solution.py:504
  73.4 1.4 %slice.229 = bf16[8,2,128]{2,1,0:T(2,128)(2,1)} slice(f32[8,8,128]{2,1,0:T(8,128)} %get-tuple-element.13), slice={[0:8], [0:2], [0:128]} | slice | bytes 8192 | tf_op jit(solution)/shard_map/slice | solution.py:496
  74.7 1.5 %copy.67 = bf16[128,256]{1,0:T(8,128)(2,1)} copy(bf16[128,256]{1,0:T(8,128)(2,1)} %get-tuple-element.59) | data formatting | bytes 131072
  76.2 0.6 copy.68
  76.8 1.9 %copy.69 = bf16[256,1024]{1,0:T(8,128)(2,1)} copy(bf16[256,1024]{1,0:T(8,128)(2,1)} %get-tuple-element.62) | data formatting | bytes 1048576
  78.8 0.8 copy.70
  (78 shorter events, 6.5 us)
Async XLA Ops:
  0.6 24.0 %copy-start = (bf16[256,1024]{1,0:T(8,128)(2,1)S(1)}, bf16[256,1024]{1,0:T(8,128)(2,1)}, u32[]{:S(2)}) copy-start(bf16[256,1024]{1,0:T(8,128)(2,1)} %param.19) | copy-start | bytes 1572868
  1.7 7.0 %copy-start.6 = (s32[4,32,8]{1,2,0:T(8,128)S(1)}, s32[4,32,8]{1,2,0:T(8,128)}, u32[]{:S(2)}) copy-start(s32[4,32,8]{1,2,0:T(8,128)} %param.22) | copy-start | bytes 12292
  2.4 11.9 %all-to-all-start = ((bf16[8,2,128]{2,1,0:T(2,128)(2,1)}), bf16[8,2,128]{2,1,0:T(2,128)(2,1)S(1)}, u32[]{:S(2)}, u32[]{:S(2)}) async-start(bf16[8,2,128]{2,1,0:T(2,128)(2,1)} %bitcast.94), calls=%async_computation | async-start | bytes 8192 | tf_op jit(solution)/shard_map/all_to_all | solution.py:454
  8.8 0.7 copy-start.10
  8.9 0.7 copy-start.7
  9.9 0.7 copy-start.11
  17.5 0.9 %copy-start.13 = (bf16[1,32,8,256]{3,2,1,0:T(8,128)(2,1)S(1)}, bf16[1,32,8,256]{3,2,1,0:T(8,128)(2,1)}, u32[]{:S(2)}) copy-start(bf16[1,32,8,256]{3,2,1,0:T(8,128)(2,1)} %param.15) | copy-start | bytes 393220
  17.5 0.9 %copy-start.14 = (bf16[128,256]{1,0:T(8,128)(2,1)S(1)}, bf16[128,256]{1,0:T(8,128)(2,1)}, u32[]{:S(2)}) copy-start(bf16[128,256]{1,0:T(8,128)(2,1)} %param.16) | copy-start | bytes 196612
  18.7 5.2 %collective-permute-start = (bf16[32,1,256]{2,1,0:T(2,128)(2,1)S(1)}, bf16[32,1,256]{2,1,0:T(2,128)(2,1)S(1)}, u32[]{:S(2)}, u32[]{:S(2)}) collective-permute-start(bf16[32,1,256]{2,1,0:T(2,128)(2,1)S(1)} %get-tuple-element.36), channel_id=1, source_target_pairs={{0,1},{1,2},{2,3},{3,4},{4,5},{5,6},{6,7},{7,0},{8,9},{9,10},{10,1... | collective-permute-start | bytes 49160 | tf_op jit(solution)/shard_map/ppermute | solution.py:277
  18.7 5.1 %collective-permute-start.1 = (bf16[32,1,256]{2,1,0:T(2,128)(2,1)S(1)}, bf16[32,1,256]{2,1,0:T(2,128)(2,1)S(1)}, u32[]{:S(2)}, u32[]{:S(2)}) collective-permute-start(bf16[32,1,256]{2,1,0:T(2,128)(2,1)S(1)} %get-tuple-element.37), channel_id=1, source_target_pairs={{1,0},{2,1},{3,2},{4,3},{5,4},{6,5},{7,6},{0,7},{9,8},{10,9},{11,1... | collective-permute-start | bytes 49160 | tf_op jit(solution)/shard_map/ppermute | solution.py:279
  24.6 0.7 copy-start.8
  25.3 0.9 %copy-start.3 = (bf16[1,32,8,256]{3,2,1,0:T(8,128)(2,1)S(1)}, bf16[1,32,8,256]{3,2,1,0:T(8,128)(2,1)}, u32[]{:S(2)}) copy-start(bf16[1,32,8,256]{3,2,1,0:T(8,128)(2,1)} %param.25) | copy-start | bytes 393220
  25.3 1.1 %copy-start.12 = (bf16[1024,256]{1,0:T(8,128)(2,1)S(1)}, bf16[1024,256]{1,0:T(8,128)(2,1)}, u32[]{:S(2)}) copy-start(bf16[1024,256]{1,0:T(8,128)(2,1)} %param.20) | copy-start | bytes 1572868
  31.3 4.3 %copy-start.2 = (bf16[256,256]{1,0:T(8,128)(2,1)}, bf16[256,256]{1,0:T(8,128)(2,1)S(1)}, u32[]{:S(2)}) copy-start(bf16[256,256]{1,0:T(8,128)(2,1)S(1)} %fusion.2) | copy-start | bytes 393220
  31.9 3.7 %copy-start.5 = (bf16[256,128]{1,0:T(8,128)(2,1)S(1)}, bf16[256,128]{1,0:T(8,128)(2,1)}, u32[]{:S(2)}) copy-start(bf16[256,128]{1,0:T(8,128)(2,1)} %param.21) | copy-start | bytes 196612
  31.9 5.3 %collective-permute-start.2 = (f32[32,1,256]{2,1,0:T(1,128)S(1)}, f32[32,1,256]{2,1,0:T(1,128)S(1)}, u32[]{:S(2)}, u32[]{:S(2)}) collective-permute-start(f32[32,1,256]{2,1,0:T(1,128)S(1)} %get-tuple-element.34), channel_id=1, source_target_pairs={{0,1},{1,2},{2,3},{3,4},{4,5},{5,6},{6,7},{7,0},{8,9},{9,10},{10,1... | collective-permute-start | bytes 98312 | tf_op jit(solution)/shard_map/ppermute | solution.py:277
  32.0 5.2 %collective-permute-start.3 = (f32[32,1,256]{2,1,0:T(1,128)S(1)}, f32[32,1,256]{2,1,0:T(1,128)S(1)}, u32[]{:S(2)}, u32[]{:S(2)}) collective-permute-start(f32[32,1,256]{2,1,0:T(1,128)S(1)} %get-tuple-element.35), channel_id=1, source_target_pairs={{1,0},{2,1},{3,2},{4,3},{5,4},{6,5},{7,6},{0,7},{9,8},{10,9},{11,1... | collective-permute-start | bytes 98312 | tf_op jit(solution)/shard_map/ppermute | solution.py:279
  37.7 1.0 %copy-start.4 = (bf16[32,8,256]{2,1,0:T(8,128)(2,1)}, bf16[32,8,256]{2,1,0:T(8,128)(2,1)S(1)}, u32[]{:S(2)}) copy-start(bf16[32,8,256]{2,1,0:T(8,128)(2,1)S(1)} %fusion.19) | copy-start | bytes 393220
  74.7 1.5 %copy-start.9 = (bf16[16,256]{1,0:T(8,128)(2,1)S(1)}, bf16[16,256]{1,0:T(8,128)(2,1)}, u32[]{:S(2)}) copy-start(bf16[16,256]{1,0:T(8,128)(2,1)} %get-tuple-element.15) | copy-start | bytes 24580
  76.8 1.9 %copy-start.1 = (bf16[1024,256]{1,0:T(8,128)(2,1)S(1)}, bf16[1024,256]{1,0:T(8,128)(2,1)}, u32[]{:S(2)}) copy-start(bf16[1024,256]{1,0:T(8,128)(2,1)} %get-tuple-element.63) | copy-start | bytes 1572868

commit v2 on v0

--- a/solution.py
+++ b/solution.py
@@ -1,12 +1,329 @@
+import functools
 import math
 
 import jax
 import jax.numpy as jnp
 from jax import lax
+from jax.experimental import pallas as pl
+from jax.experimental.pallas import tpu as pltpu
 from jax.sharding import PartitionSpec as P
 
 SUBDIVISION = 4
 KS = 3
+LANES = 128
+SLABS = 3
+MESH = pl.DeviceIdType.MESH
+
+
+def pack_plan(shapes):
+    plan, at = [], 0
+    for which, (rows, cols) in enumerate(shapes):
+        for col in range(0, cols, LANES):
+            plan.append((which, col, at, rows))
+            at += rows
+    return plan, at
+
+
+def reduce_kernel(
+    scale,
+    ne,
+    nt,
+    rows,
+    plan,
+    used,
+    up_ref,
+    down_ref,
+    force_ref,
+    conv_ref,
+    gain_ref,
+    therm_ref,
+    whole,
+    therm_out,
+    small,
+    packed,
+    from_core,
+    halves,
+    from_ens,
+    part,
+    from_z,
+    therm_in,
+    t_send,
+    t_recv,
+    a_send,
+    a_recv,
+    b_send,
+    b_recv,
+    c_send,
+    c_recv,
+    d_send,
+    d_recv,
+    e_send,
+    e_recv,
+    f_send,
+    f_recv,
+):
+    nz = nt // 2
+    block = nz * rows
+    slab = 2 * ne * block
+    ens = lax.axis_index("ens")
+    tile = lax.axis_index("tile")
+    z = tile // 2
+    core = tile % 2
+    other = 1 - core
+    mate = {"tile": z * 2 + other}
+
+    def send(src, dst, s_sem, r_sem, device):
+        copy = pltpu.make_async_remote_copy(
+            src_ref=src,
+            dst_ref=dst,
+            send_sem=s_sem,
+            recv_sem=r_sem,
+            device_id=device,
+            device_id_type=MESH,
+        )
+        copy.start()
+        return copy
+
+    def at_block(s, h, e):
+        return pl.ds(pl.multiple_of(s * slab + (h * ne + e) * block, 16), block)
+
+    def at_chunk(where):
+        return pl.ds(pl.multiple_of(where * rows, 16), rows)
+
+    barrier = pltpu.get_barrier_semaphore()
+    for o in range(1, nt):
+        pl.semaphore_signal(
+            barrier, inc=1, device_id={"tile": (tile + o) % nt}, device_id_type=MESH
+        )
+    for o in range(1, ne):
+        pl.semaphore_signal(
+            barrier, inc=1, device_id={"ens": (ens + o) % ne}, device_id_type=MESH
+        )
+
+    taps = conv_ref.shape[0]
+    small[...] = jnp.zeros_like(small)
+    small[0:taps, :] = conv_ref[...]
+    small[taps : taps + 1, :] = gain_ref[...]
+    ins = (up_ref, down_ref, force_ref, small)
+    if used < SLABS * slab:
+        packed[used : SLABS * slab, :] = jnp.zeros((SLABS * slab - used, LANES), jnp.bfloat16)
+
+    order = list(range(1, ne)) + [0]
+    a_copies = [[] for _ in range(SLABS)]
+
+    def send_slab(s):
+        for o in order:
+            e = (ens + o) % ne
+            a_copies[s].append(
+                send(
+                    packed.at[at_block(s, other, e)],
+                    from_core.at[s, o],
+                    a_send.at[s, o],
+                    a_recv.at[s, o],
+                    mate,
+                )
+            )
+
+    ready = 0
+    for which, col, at, count in plan:
+        packed[at : at + count, :] = ins[which][:, col : col + LANES].astype(jnp.bfloat16)
+        while ready < SLABS and at + count >= min((ready + 1) * slab, used):
+            if ready == 0:
+                pl.semaphore_wait(barrier, nt - 1 + ne - 1)
+            send_slab(ready)
+            ready += 1
+
+    t_copies = []
+    for o in range(1, nt):
+        to = (tile + o) % nt
+        t_copies.append(
+            send(
+                therm_ref.at[to],
+                therm_in.at[o],
+                t_send.at[o],
+                t_recv.at[o],
+                {"tile": to},
+            )
+        )
+    b_copies = [[] for _ in range(SLABS)]
+    for s in range(SLABS):
+        for o, copy in zip(order, a_copies[s]):
+            e = (ens + o) % ne
+            copy.wait_recv()
+            halves[s, o] = (
+                packed[at_block(s, core, e), :].astype(jnp.float32)
+                + from_core[s, o].astype(jnp.float32)
+            ).astype(jnp.bfloat16)
+            if o:
+                b_copies[s].append(
+                    send(
+                        halves.at[s, o],
+                        from_ens.at[s, o],
+                        b_send.at[s, o],
+                        b_recv.at[s, o],
+                        {"ens": e},
+                    )
+                )
+    c_copies = [[] for _ in range(SLABS)]
+    for s in range(SLABS):
+        total = halves[s, 0].astype(jnp.float32)
+        for o, copy in zip(range(1, ne), b_copies[s]):
+            copy.wait_recv()
+            total = total + from_ens[s, o].astype(jnp.float32)
+        part[s] = total.astype(jnp.bfloat16)
+        for o in range(1, nz):
+            to = (z + o) % nz
+            c_copies[s].append(
+                send(
+                    part.at[s, at_chunk(to)],
+                    from_z.at[s, o],
+                    c_send.at[s, o],
+                    c_recv.at[s, o],
+                    {"tile": to * 2 + core},
+                )
+            )
+    d_copies = [[] for _ in range(SLABS)]
+    for s in range(SLABS):
+        mine = part[s, at_chunk(z), :].astype(jnp.float32)
+        for o, copy in zip(range(1, nz), c_copies[s]):
+            copy.wait_recv()
+            mine = mine + from_z[s, o].astype(jnp.float32)
+        spot = at_chunk(((s * 2 + core) * ne + ens) * nz + z)
+        whole[spot, :] = (mine * scale).astype(jnp.bfloat16)
+        for o in range(1, nz):
+            to = (z + o) % nz
+            d_copies[s].append(
+                send(
+                    whole.at[spot],
+                    whole.at[spot],
+                    d_send.at[s, o],
+                    d_recv.at[s, o],
+                    {"tile": to * 2 + core},
+                )
+            )
+    e_copies = [[] for _ in range(SLABS)]
+    f_copies = []
+    for s in range(SLABS):
+        for copy in d_copies[s]:
+            copy.wait_recv()
+        own = at_block(s, core, ens)
+        for o in range(1, ne):
+            e_copies[s].append(
+                send(
+                    whole.at[own],
+                    whole.at[own],
+                    e_send.at[s, o],
+                    e_recv.at[s, o],
+                    {"ens": (ens + o) % ne},
+                )
+            )
+        f_copies.append(send(whole.at[own], whole.at[own], f_send.at[s, 0], f_recv.at[s, 0], mate))
+    for s in range(SLABS):
+        for o, copy in zip(range(1, ne), e_copies[s]):
+            copy.wait_recv()
+            theirs = at_block(s, core, (ens + ne - o) % ne)
+            f_copies.append(
+                send(whole.at[theirs], whole.at[theirs], f_send.at[s, o], f_recv.at[s, o], mate)
+            )
+    therm_out[tile] = therm_ref[tile]
+    for o, copy in zip(range(1, nt), t_copies):
+        copy.wait_recv()
+        therm_out[(tile + nt - o) % nt] = therm_in[o]
+    for copy in f_copies:
+        copy.wait_recv()
+    sent = t_copies + f_copies
+    for group in (a_copies, b_copies, c_copies, d_copies, e_copies):
+        for copies in group:
+            sent = sent + copies
+    for copy in sent:
+        copy.wait_send()
+
+
+def unpack_kernel(
+    plan, whole, therm, up_out, down_out, force_out, conv_out, gain_out, therm_out, strip, sems
+):
+    outs = (up_out, down_out, force_out)
+    copies = []
+    for i, (which, col, at, count) in enumerate(plan):
+        if which < len(outs):
+            copies.append(
+                pltpu.make_async_copy(
+                    whole.at[at : at + count, :],
+                    outs[which].at[:, col : col + LANES],
+                    sems.at[i],
+                )
+            )
+            copies[-1].start()
+    taps = conv_out.shape[0]
+    for which, col, at, count in plan:
+        if which == len(outs):
+            rows = whole[at : at + count, :].astype(jnp.float32)
+            conv_out[:, col : col + LANES] = rows[:taps].astype(jnp.bfloat16)
+            gain_out[:, col : col + LANES] = rows[taps : taps + 1].astype(jnp.bfloat16)
+    tiles, columns, _ = therm.shape
+    for t in range(tiles):
+        strip[t * columns : (t + 1) * columns, :] = therm[t]
+    therm_out[0] = strip[...].astype(jnp.bfloat16)
+    for copy in copies:
+        copy.wait()
+
+
+def reduce_gradients(up, down, force, conv, gain, therm, scale):
+    ne, nt = lax.axis_size("ens"), lax.axis_size("tile")
+    nz = nt // 2
+    taps, features = conv.shape
+    small_rows = -(-(taps + 1) // 16) * 16
+    plan, used = pack_plan([up.shape, down.shape, force.shape, (small_rows, features)])
+    rows = -(-used // (SLABS * 2 * ne * nz * 16)) * 16
+    block = nz * rows
+    bf16 = jnp.bfloat16
+    dma = pltpu.SemaphoreType.DMA
+    vmem = pl.BlockSpec(memory_space=pltpu.VMEM)
+    anywhere = pl.BlockSpec(memory_space=pl.ANY)
+    tiles, columns, quantity = therm.shape
+    whole, therm = pl.pallas_call(
+        functools.partial(reduce_kernel, scale, ne, nt, rows, plan, used),
+        out_shape=[
+            jax.ShapeDtypeStruct((SLABS * 2 * ne * block, LANES), bf16),
+            jax.ShapeDtypeStruct(therm.shape, therm.dtype),
+        ],
+        in_specs=[vmem] * 6,
+        out_specs=[vmem] * 2,
+        scratch_shapes=[
+            pltpu.VMEM((small_rows, features), jnp.float32),
+            pltpu.VMEM((SLABS * 2 * ne * block, LANES), bf16),
+            pltpu.VMEM((SLABS, ne, block, LANES), bf16),
+            pltpu.VMEM((SLABS, ne, block, LANES), bf16),
+            pltpu.VMEM((SLABS, ne, block, LANES), bf16),
+            pltpu.VMEM((SLABS, block, LANES), bf16),
+            pltpu.VMEM((SLABS, nz, rows, LANES), bf16),
+            pltpu.VMEM(therm.shape, therm.dtype),
+        ]
+        + [dma((nt,)), dma((nt,))]
+        + [dma((SLABS, ne)), dma((SLABS, ne))] * 2
+        + [dma((SLABS, nz)), dma((SLABS, nz))] * 2
+        + [dma((SLABS, ne)), dma((SLABS, ne))] * 2,
+        compiler_params=pltpu.CompilerParams(collective_id=1, has_side_effects=True),
+        name="reduce_gradients",
+    )(up, down, force, conv, gain, therm)
+    return pl.pallas_call(
+        functools.partial(unpack_kernel, plan),
+        out_shape=[
+            jax.ShapeDtypeStruct(up.shape, bf16),
+            jax.ShapeDtypeStruct(down.shape, bf16),
+            jax.ShapeDtypeStruct(force.shape, bf16),
+            jax.ShapeDtypeStruct(conv.shape, bf16),
+            jax.ShapeDtypeStruct(gain.shape, bf16),
+            jax.ShapeDtypeStruct((1, tiles * columns, quantity), bf16),
+        ],
+        in_specs=[vmem] * 2,
+        out_specs=[anywhere] * 3 + [vmem] * 3,
+        scratch_shapes=[
+            pltpu.VMEM((tiles * columns, quantity), jnp.float32),
+            dma((len(plan),)),
+        ],
+        name="unpack_gradients",
+    )(whole, therm)
 
 
 def extended(cells, sides, width):
@@ -214,9 +531,6 @@
             pad_grad_cols,
         )
     )
-    thermal_strip_slice = lax.all_to_all(
-        thermal_lowres_field, "tile", split_axis=0, concat_axis=1, tiled=True
-    )
     cell_total = (
         lax.axis_size("ens")
         * lax.axis_size("tile")
@@ -225,19 +539,24 @@
     )
     grad_scale = 1.0 / math.sqrt(cell_total)
     grad_force, grad_conv, grad_gain, grad_up, grad_down = derivative_sequence
-    accumulated_result = lax.psum(
-        (grad_force, grad_conv, grad_gain, grad_up, grad_down), ("ens", "tile")
-    )
-    scaled = [(values * grad_scale).astype(jnp.bfloat16) for values in accumulated_result]
+    up, down, force, conv, gain, thermal_strip_slice = reduce_gradients(
+        grad_up,
+        grad_down,
+        grad_force,
+        grad_conv,
+        grad_gain.reshape(1, -1),
+        thermal_lowres_field.astype(jnp.float32),
+        grad_scale,
+    )
     return (
         marine_successor_latent[None],
         thermal_strip_slice[None],
         marine_latent_adjoint[None],
-        scaled[0],
-        scaled[1],
-        scaled[2],
-        scaled[3],
-        scaled[4],
+        force,
+        conv,
+        gain.reshape(-1),
+        up,
+        down,
     )
 
 

time: 194 us -> 72.7 us (0.37)
  waiting for transfers between devices: 93.1 us -> 1.66 us
  blocking collectives: 41.1 us -> 0 us
  Pallas kernels: 0 us -> 32.7 us
  between operations: 14.3 us -> 0.91 us
  starting transfers between devices: 18.4 us -> 13.6 us
  local copies, waits for them, and re-layouts: 10.1 us -> 7.47 us
    psum x1 -> x0, waiting for transfers between devices: 88.8 us -> none  [body(): lax.psum((grad_force, grad_conv, grad_gain, grad_up, grad_down), ('ens',...]
    psum x1 -> x0, blocking collectives: 41.1 us -> none  [body(): lax.psum((grad_force, grad_conv, grad_gain, grad_up, grad_down), ('ens',...]
    pallas_call x0 -> x2, Pallas kernels: none -> 32.7 us  [the longest x1 29.7 us: reduce_gradients(): pl.pallas_call(functools.partial(reduce_kernel, scale, ne, nt, rows, plan...]
    convert_element_type x6 -> x1, other arithmetic: 6.43 us -> 0.68 us  [body(): thermal_lowres_field.astype(jnp.float32)]
    all_to_all x1 -> x0, starting transfers between devices: 4.82 us -> none  [body(): lax.all_to_all(thermal_lowres_field, 'tile', split_axis=0, concat_axis=1,...]
    unnamed x32 -> x21, local copies, waits for them, and re-layouts: 5.81 us -> 1 us
    all_to_all x1, waiting for transfers between devices: 2.79 us -> 0.3 us  [body(): lax.all_to_all(fluxes, 'tile', split_axis=1, concat_axis=0, tiled=True)]
  transfers between devices with their start and end apart: 7 -> 5, of which waited for: 5 -> 2; matrix products, arithmetic and copies ran while one was open for 2% -> 10% of each run, Pallas kernels for 0% -> 0%
where the time goes in v2:
time: 72.7 us; the launch traced here: 72 us
  Pallas kernels  32.7 us (45%)
  starting transfers between devices  13.6 us (19%)
  matrix products  8.13 us (11%)
  other arithmetic  7.53 us (10%)
  local copies, waits for them, and re-layouts  7.47 us (10%)
  waiting for transfers between devices  1.66 us (2%)
  between operations  0.91 us (1%)
    pallas_call x1, Pallas kernels, reduce_gradients(): pl.pallas_call(functools.partial(reduce_kernel, scale, ne, nt, rows, plan...  29.7 us
    ppermute x2, starting transfers between devices, extended(): lax.ppermute(head, axis, [((i + 1) % count, i) for i in range(count)])  6.76 us
    all_to_all x1, starting transfers between devices, body(): lax.all_to_all(fluxes, 'tile', split_axis=1, concat_axis=0, tiled=True)  6.35 us
    gather x1, local copies, waits for them, and re-layouts, regrid(): picked = jnp.take(flat_fluxes, cell_ids, axis=0).astype(jnp.float32)  3.2 us
    pallas_call x1, Pallas kernels, reduce_gradients(): pl.pallas_call(functools.partial(unpack_kernel, plan), out_shape=[jax.Sha...  2.97 us
    dot_general x1, matrix products, marine_update_kernel(): jnp.dot(hidden.T, masked_cot, preferred_element_type=jnp.float32)  1.59 us
    dot_general x1, matrix products, marine_update_kernel(): grad_up = jnp.dot(normed.T, pre_cot, preferred_element_type=jnp.float32)  1.47 us
  transfers between devices with their start and end apart: 5, of which 2 were waited for; matrix products, arithmetic and copies ran while one was open for 10% of the time, Pallas kernels for 0%

profile of v2, /device:TPU:0, one launch (start us, length us, event | category | flops | bytes accessed | tf_op | source)
XLA Modules:
  0.0 72.0 jit_solution(4025292469768996124)
XLA Ops:
  0.6 1.1 %fusion.3 = bf16[1,16,128]{2,1,0:T(8,128)(2,1)S(1)} fusion(bf16[384,128]{1,0:T(8,128)(2,1)} %param.14, bf16[1,1,16,384]{3,2,1,0:T(8,128)(2,1)} %param.13), kind=kOutput, calls=%fused_computation.10 | convolution fusion | flops 1574912 | bytes 114688 | tf_op jit(solution)/shard_map/dot_general | solution.py:509
  1.8 0.6 copy.62
  2.4 6.4 %all-to-all-start = ((bf16[8,2,128]{2,1,0:T(2,128)(2,1)}), bf16[8,2,128]{2,1,0:T(2,128)(2,1)S(1)}, u32[]{:S(2)}, u32[]{:S(2)}) async-start(bf16[8,2,128]{2,1,0:T(2,128)(2,1)} %bitcast.93), calls=%async_computation | async-start | bytes 8192 | tf_op jit(solution)/shard_map/all_to_all | solution.py:513
  8.7 0.7 %compare_select_fusion = s32[4,32,8]{1,2,0:T(8,128)S(1)} fusion(s32[4,32,8]{1,2,0:T(8,128)} %param.22), kind=kLoop, calls=%fused_computation.76 | loop fusion | flops 3072 | bytes 8192 | tf_op jit(solution)/shard_map/jit(_take)/jit(_where)/select_n | solution.py:352
  9.4 0.7 %compare_and_fusion = pred[4,32,8]{1,2,0:T(8,128)(4,1)S(1)} fusion(s32[4,32,8]{1,2,0:T(8,128)} %param.22), kind=kLoop, calls=%fused_computation.78 | loop fusion | flops 6144 | bytes 5120 | tf_op jit(solution)/shard_map/jit(_take)/and | solution.py:352
  10.4 1.0 %fusion.45 = (f32[1,256]{1,0:T(1,128)S(1)}, f32[1,256]{1,0:T(1,128)S(1)}, f32[1,256]{1,0:T(1,128)S(1)}, f32[1,256]{1,0:T(1,128)S(1)}, f32[1,256]{1,0:T(1,128)S(1...) fusion(f32[9,256]{1,0:T(8,128)} %param.17), kind=kLoop, calls=%fused_computation.95 | loop fusion | bytes 18432 | tf_op jit(solution)/shard_map/slice | solution.py:387
  11.4 0.7 %convert_reduce_fusion = f32[32,8]{0,1:T(8,128)S(1)} fusion(s32[4,32,8]{1,2,0:T(8,128)} %param.23), kind=kLoop, calls=%fused_computation.88 | loop fusion | flops 1792 | bytes 5120 | tf_op jit(solution)/shard_map/reduce_sum | solution.py:355
  12.1 0.7 convert_element_type.85
  13.1 0.7 convert_element_type.82
  14.3 3.2 %gather_fusion = bf16[1024,128]{1,0:T(8,128)(2,1)S(1)} fusion(bf16[16,128]{1,0:T(8,128)(2,1)S(1)} %bitcast.94, s32[1024]{0:T(1024)S(1)} %broadcast_clamp_fusion), kind=kCustom, calls=%fused_computation | custom fusion | bytes 528384 | tf_op jit(solution)/shard_map/jit(_take)/gather | solution.py:352
  18.4 3.3 %collective-permute-start.1 = (bf16[32,1,256]{2,1,0:T(2,128)(2,1)S(1)}, bf16[32,1,256]{2,1,0:T(2,128)(2,1)S(1)}, u32[]{:S(2)}, u32[]{:S(2)}) collective-permute-start(bf16[32,1,256]{2,1,0:T(2,128)(2,1)S(1)} %get-tuple-element.43), channel_id=1, source_target_pairs={{1,0},{2,1},{3,2},{4,3},{5,4},{6,5},{7,6},{0,7},{9,8},{10,9},{11,1... | collective-permute-start | bytes 49160 | tf_op jit(solution)/shard_map/ppermute | solution.py:338
  22.0 1.4 %collective-permute-done = bf16[32,1,256]{2,1,0:T(2,128)(2,1)S(1)} collective-permute-done((bf16[32,1,256]{2,1,0:T(2,128)(2,1)S(1)}, bf16[32,1,256]{2,1,0:T(2,128)(2,1)S(1)}, u32[]{:S(2)}, u32[]{:S(2)}) %collective-permute-start) | collective-permute-done | bytes 16416 | tf_op jit(solution)/shard_map/ppermute | solution.py:336
  24.9 0.9 %fusion.10 = bf16[256,1024]{1,0:T(8,128)(2,1)S(1)} fusion(f32[256,1024]{1,0:T(8,128)S(1)} %fusion.40, bf16[1024,256]{1,0:T(8,128)(2,1)S(1)} %copy-done.6, bf16[1,32,8,256]{3,2,1,0:T(8,128)(2,1)S(1)} %copy-done.2, f32[256]{0:T(256)S(1)} %mul.301), kind=kOutput, calls=%fused_computation.17 | convolution fusion | flops 139657216 | bytes 2229248 | tf_op jit(solution)/shard_map/dot_general | solution.py:432
  25.7 0.9 %multiply_reduce_fusion.1 = (f32[256]{0:T(256)}, f32[256]{0:T(256)S(1)}, f32[256,256]{1,0:T(8,128)S(1)}) fusion(f32[32,8,256]{2,1,0:T(8,128)S(1)} %get-tuple-element.39, f32[256]{0:T(256)S(1)} %rsqrt.10, f32[256]{0:T(256)S(1)} %div.41, f32[256]{0:T(256)S(1)} %copy-done.5, bf16[256,1024]{1,0:T(8,128)(2,1)S(1)} %fusion.10, bf16[256,1024]{1,0:T(8,128)(2,1)S(1)} %copy-done), kind=kOutput, calls=%fused_computation.57 | convolution fusion | flops 134675968 | bytes 1577984 | tf_op jit(solution)/shard_map/dot_general | solution.py:435
  26.7 1.5 %fusion.39.up_ref = f32[256,1024]{1,0:T(8,128)} fusion(bf16[256,1024]{1,0:T(8,128)(2,1)S(1)} %fusion.10, f32[32,8,256]{2,1,0:T(8,128)S(1)} %get-tuple-element.39, f32[256]{0:T(256)S(1)} %copy-done.5, f32[256]{0:T(256)S(1)} %rsqrt.10, f32[256]{0:T(256)S(1)} %div.41), kind=kOutput, calls=%fused_computation.89 | convolution fusion | flops 134479872 | bytes 1838080 | tf_op jit(solution)/shard_map/dot_general | solution.py:434
  28.1 1.6 %fusion.31.down_ref = f32[1024,256]{1,0:T(8,128)} fusion(bf16[1,32,8,256]{3,2,1,0:T(8,128)(2,1)S(1)} %copy-done.2, f32[256]{0:T(256)S(1)} %mul.301, f32[256,1024]{1,0:T(8,128)S(1)} %fusion.40), kind=kOutput, calls=%fused_computation.74 | convolution fusion | flops 136773632 | bytes 2229248 | tf_op jit(solution)/shard_map/dot_general | solution.py:431
  29.7 0.5 fusion.2
  31.1 3.4 %collective-permute-start.3 = (f32[32,1,256]{2,1,0:T(1,128)S(1)}, f32[32,1,256]{2,1,0:T(1,128)S(1)}, u32[]{:S(2)}, u32[]{:S(2)}) collective-permute-start(f32[32,1,256]{2,1,0:T(1,128)S(1)} %get-tuple-element.41), channel_id=1, source_target_pairs={{1,0},{2,1},{3,2},{4,3},{5,4},{6,5},{7,6},{0,7},{9,8},{10,9},{11,1... | collective-permute-start | bytes 98312 | tf_op jit(solution)/shard_map/ppermute | solution.py:338
  34.7 0.7 fusion.38.therm_ref
  35.4 1.2 %stack.39.conv_ref = f32[9,256]{1,0:T(8,128)} concatenate(f32[1,256]{1,0:T(1,128)S(1)} %bitcast.126, f32[1,256]{1,0:T(1,128)S(1)} %bitcast.125, f32[1,256]{1,0:T(1,128)S(1)} %bitcast.124, f32[1,256]{1,0:T(1,128)S(1)} %bitcast.123, f32[1,256]{1,0:T(1,128)S(1)} %bitcast.122, f32[1,256]{1,0:T(1,128)S(1)} %bitcast.121, f32[1,256]{1,0:T(1,128)S(1)} %bitcast.120, ...), dimensions={0} | concatenate | bytes 18432 | tf_op jit(solution)/shard_map/stack | solution.py:473
  37.1 1.0 %convolution_bitcast_fusion.force_ref = f32[128,256]{1,0:T(8,128)} fusion(bf16[32,8,256]{2,1,0:T(8,128)(2,1)S(1)} %fusion.19, f32[32,8,128]{2,1,0:T(8,128)S(1)} %multiply_reduce_fusion, f32[32,8]{1,0:T(8,128)S(1)} %copy.54), kind=kOutput, calls=%fused_computation.8 | convolution fusion | flops 16842752 | bytes 394240 | tf_op jit(solution)/shard_map/dot_general | solution.py:468
  38.1 29.7 %reduce_gradients.1 = (bf16[4608,128]{1,0:T(8,128)(2,1)}, f32[8,2,128]{2,1,0:T(2,128)}) custom-call(f32[256,1024]{1,0:T(8,128)} %fusion.39.up_ref, f32[1024,256]{1,0:T(8,128)} %fusion.31.down_ref, f32[128,256]{1,0:T(8,128)} %convolution_bitcast_fusion.force_ref, f32[9,256]{1,0:T(8,128)} %stack.39.conv_ref, f32[1,256]{1,0:T(1,128)} %bitcast.128, ...), custom_call_target="tpu_custom_call" | custom-call | tf_op jit(solution)/shard_map/reduce_gradients/pallas_call | solution.py:284
  67.8 3.0 %unpack_gradients.1 = (bf16[256,1024]{1,0:T(8,128)(2,1)}, bf16[1024,256]{1,0:T(8,128)(2,1)}, bf16[128,256]{1,0:T(8,128)(2,1)}, bf16[9,256]{1,0:T(8,128)(2,1)}, b...) custom-call(bf16[4608,128]{1,0:T(8,128)(2,1)} %get-tuple-element.16.whole, f32[8,2,128]{2,1,0:T(2,128)} %get-tuple-element.17.therm), custom_call_target="tpu_custom_call" | custom-call | tf_op jit(solution)/shard_map/unpack_gradients/pallas_call | solution.py:309
  70.8 1.2 %reduce.2 = bf16[256]{0:T(256)(128)(2,1)} reduce(bf16[1,256]{1,0:T(2,128)(2,1)} %get-tuple-element.21, bf16[]{:T(256)} %constant.52), dimensions={0}, to_apply=%get-tuple-element.21.reduce_sub_computation | reduce | bytes 1026 | tf_op jit(solution)/shard_map/unpack_gradients/pallas_call | solution.py:309
  (60 shorter events, 5.0 us)
Async XLA Ops:
  0.6 23.5 %copy-start = (bf16[256,1024]{1,0:T(8,128)(2,1)S(1)}, bf16[256,1024]{1,0:T(8,128)(2,1)}, u32[]{:S(2)}) copy-start(bf16[256,1024]{1,0:T(8,128)(2,1)} %param.19) | copy-start | bytes 1572868
  2.4 11.9 %all-to-all-start = ((bf16[8,2,128]{2,1,0:T(2,128)(2,1)}), bf16[8,2,128]{2,1,0:T(2,128)(2,1)S(1)}, u32[]{:S(2)}, u32[]{:S(2)}) async-start(bf16[8,2,128]{2,1,0:T(2,128)(2,1)} %bitcast.93), calls=%async_computation | async-start | bytes 8192 | tf_op jit(solution)/shard_map/all_to_all | solution.py:513
  14.2 3.6 %copy-start.7 = (bf16[1,32,8,256]{3,2,1,0:T(8,128)(2,1)S(1)}, bf16[1,32,8,256]{3,2,1,0:T(8,128)(2,1)}, u32[]{:S(2)}) copy-start(bf16[1,32,8,256]{3,2,1,0:T(8,128)(2,1)} %param.15) | copy-start | bytes 393220
  14.2 3.6 %copy-start.8 = (bf16[128,256]{1,0:T(8,128)(2,1)S(1)}, bf16[128,256]{1,0:T(8,128)(2,1)}, u32[]{:S(2)}) copy-start(bf16[128,256]{1,0:T(8,128)(2,1)} %param.16) | copy-start | bytes 196612
  18.1 5.2 %collective-permute-start = (bf16[32,1,256]{2,1,0:T(2,128)(2,1)S(1)}, bf16[32,1,256]{2,1,0:T(2,128)(2,1)S(1)}, u32[]{:S(2)}, u32[]{:S(2)}) collective-permute-start(bf16[32,1,256]{2,1,0:T(2,128)(2,1)S(1)} %get-tuple-element.42), channel_id=1, source_target_pairs={{0,1},{1,2},{2,3},{3,4},{4,5},{5,6},{6,7},{7,0},{8,9},{9,10},{10,1... | collective-permute-start | bytes 49160 | tf_op jit(solution)/shard_map/ppermute | solution.py:336
  18.4 4.9 %collective-permute-start.1 = (bf16[32,1,256]{2,1,0:T(2,128)(2,1)S(1)}, bf16[32,1,256]{2,1,0:T(2,128)(2,1)S(1)}, u32[]{:S(2)}, u32[]{:S(2)}) collective-permute-start(bf16[32,1,256]{2,1,0:T(2,128)(2,1)S(1)} %get-tuple-element.43), channel_id=1, source_target_pairs={{1,0},{2,1},{3,2},{4,3},{5,4},{6,5},{7,6},{0,7},{9,8},{10,9},{11,1... | collective-permute-start | bytes 49160 | tf_op jit(solution)/shard_map/ppermute | solution.py:338
  23.5 0.7 copy-start.5
  23.8 0.9 %copy-start.2 = (bf16[1,32,8,256]{3,2,1,0:T(8,128)(2,1)S(1)}, bf16[1,32,8,256]{3,2,1,0:T(8,128)(2,1)}, u32[]{:S(2)}) copy-start(bf16[1,32,8,256]{3,2,1,0:T(8,128)(2,1)} %param.25) | copy-start | bytes 393220
  23.8 1.1 %copy-start.6 = (bf16[1024,256]{1,0:T(8,128)(2,1)S(1)}, bf16[1024,256]{1,0:T(8,128)(2,1)}, u32[]{:S(2)}) copy-start(bf16[1024,256]{1,0:T(8,128)(2,1)} %param.20) | copy-start | bytes 1572868
  30.2 4.3 %copy-start.1 = (bf16[256,256]{1,0:T(8,128)(2,1)}, bf16[256,256]{1,0:T(8,128)(2,1)S(1)}, u32[]{:S(2)}) copy-start(bf16[256,256]{1,0:T(8,128)(2,1)S(1)} %fusion.2) | copy-start | bytes 393220
  30.5 4.0 %copy-start.4 = (bf16[256,128]{1,0:T(8,128)(2,1)S(1)}, bf16[256,128]{1,0:T(8,128)(2,1)}, u32[]{:S(2)}) copy-start(bf16[256,128]{1,0:T(8,128)(2,1)} %param.21) | copy-start | bytes 196612
  30.9 5.8 %collective-permute-start.2 = (f32[32,1,256]{2,1,0:T(1,128)S(1)}, f32[32,1,256]{2,1,0:T(1,128)S(1)}, u32[]{:S(2)}, u32[]{:S(2)}) collective-permute-start(f32[32,1,256]{2,1,0:T(1,128)S(1)} %get-tuple-element.40), channel_id=1, source_target_pairs={{0,1},{1,2},{2,3},{3,4},{4,5},{5,6},{6,7},{7,0},{8,9},{9,10},{10,1... | collective-permute-start | bytes 98312 | tf_op jit(solution)/shard_map/ppermute | solution.py:336
  31.1 5.6 %collective-permute-start.3 = (f32[32,1,256]{2,1,0:T(1,128)S(1)}, f32[32,1,256]{2,1,0:T(1,128)S(1)}, u32[]{:S(2)}, u32[]{:S(2)}) collective-permute-start(f32[32,1,256]{2,1,0:T(1,128)S(1)} %get-tuple-element.41), channel_id=1, source_target_pairs={{1,0},{2,1},{3,2},{4,3},{5,4},{6,5},{7,6},{0,7},{9,8},{10,9},{11,1... | collective-permute-start | bytes 98312 | tf_op jit(solution)/shard_map/ppermute | solution.py:338
  37.1 30.7 %copy-start.3 = (bf16[32,8,256]{2,1,0:T(8,128)(2,1)}, bf16[32,8,256]{2,1,0:T(8,128)(2,1)S(1)}, u32[]{:S(2)}) copy-start(bf16[32,8,256]{2,1,0:T(8,128)(2,1)S(1)} %fusion.19) | copy-start | bytes 393220

commit v3 on v2

--- a/solution.py
+++ b/solution.py
@@ -326,6 +326,150 @@
     )(whole, therm)
 
 
+def mix_kernel(
+    nt,
+    cols,
+    air_ref,
+    exchange_ref,
+    weights_ref,
+    latent_ref,
+    driver_ref,
+    forcing_out,
+    mixed_out,
+    left_out,
+    right_out,
+    flux,
+    slabs,
+    strip_in,
+    strip,
+    state,
+    edges,
+    s_send,
+    s_recv,
+    h_send,
+    h_recv,
+):
+    tile = lax.axis_index("tile")
+    bf16, f32 = jnp.bfloat16, jnp.float32
+    barrier = pltpu.get_barrier_semaphore()
+    for o in range(1, nt):
+        pl.semaphore_signal(
+            barrier, inc=1, device_id={"tile": (tile + o) % nt}, device_id_type=MESH
+        )
+    flux[...] = (
+        jnp.dot(air_ref[...], exchange_ref[...], preferred_element_type=f32)
+        .astype(bf16)
+        .astype(f32)
+    )
+    share = slabs.shape[1]
+    for t in range(nt):
+        slabs[t] = flux[t * share : (t + 1) * share, :]
+    pl.semaphore_wait(barrier, nt - 1)
+    copies = []
+    for o in range(1, nt):
+        to = (tile + o) % nt
+        copies.append(
+            pltpu.make_async_remote_copy(
+                src_ref=slabs.at[to],
+                dst_ref=strip_in.at[tile],
+                send_sem=s_send.at[o],
+                recv_sem=s_recv.at[o],
+                device_id={"tile": to},
+                device_id_type=MESH,
+            )
+        )
+        copies[-1].start()
+    strip_in[tile] = slabs[tile]
+    weights = weights_ref[...]
+    over_sites = (((0,), (0,)), ((), ()))
+    total = lax.dot_general(
+        weights,
+        jnp.ones((weights.shape[0], strip.shape[1]), bf16),
+        over_sites,
+        preferred_element_type=f32,
+    )
+    for copy in copies:
+        copy.wait_recv()
+    for t in range(nt):
+        strip[t * share : (t + 1) * share, :] = strip_in[t]
+    weighted = lax.dot_general(
+        weights, strip[...].astype(bf16), over_sites, preferred_element_type=f32
+    )
+    forcing = (weighted / total).astype(bf16)
+    forcing_out[...] = forcing
+    mixed = (
+        latent_ref[...].astype(f32)
+        + jnp.dot(forcing, driver_ref[...], preferred_element_type=f32)
+    ).astype(bf16)
+    for lane in range(0, mixed.shape[1], LANES):
+        state[lane // LANES] = mixed[:, lane : lane + LANES].astype(f32)
+    rows = edges.shape[1]
+    for side, column in ((0, cols - 1), (1, 0)):
+        for lane in range(0, mixed.shape[1], LANES):
+            edges[side, :, lane : lane + LANES] = state[
+                lane // LANES, pl.ds(column, rows, stride=cols), :
+            ].astype(bf16)
+    hops = ((0, left_out, (tile + 1) % nt), (1, right_out, (tile + nt - 1) % nt))
+    halos = []
+    for side, out, to in hops:
+        halos.append(
+            pltpu.make_async_remote_copy(
+                src_ref=edges.at[side],
+                dst_ref=out,
+                send_sem=h_send.at[side],
+                recv_sem=h_recv.at[side],
+                device_id={"tile": to},
+                device_id_type=MESH,
+            )
+        )
+        halos[-1].start()
+    mixed_out[...] = mixed
+    for copy in halos:
+        copy.wait_recv()
+    for copy in copies + halos:
+        copy.wait_send()
+
+
+def mix_states(band, exchange, sites, margin, latent, driver):
+    nt = lax.axis_size("tile")
+    rows, cols, features = latent.shape
+    quantity = exchange.shape[1]
+    places = band.shape[0]
+    cells = rows * cols
+    flat_sites = sites.reshape(sites.shape[0], 1, cells)
+    flat_margin = margin.reshape(margin.shape[0], 1, cells)
+    names = lax.broadcasted_iota(jnp.int32, (1, places, 1), 1)
+    weights = jnp.sum(jnp.where(flat_sites == names, flat_margin, 0), axis=0)
+    bf16, f32 = jnp.bfloat16, jnp.float32
+    dma = pltpu.SemaphoreType.DMA
+    vmem = pl.BlockSpec(memory_space=pltpu.VMEM)
+    return pl.pallas_call(
+        functools.partial(mix_kernel, nt, cols),
+        out_shape=[
+            jax.ShapeDtypeStruct((cells, quantity), bf16),
+            jax.ShapeDtypeStruct((cells, features), bf16),
+            jax.ShapeDtypeStruct((rows, features), bf16),
+            jax.ShapeDtypeStruct((rows, features), bf16),
+        ],
+        in_specs=[vmem] * 5,
+        out_specs=[vmem] * 4,
+        scratch_shapes=[
+            pltpu.VMEM((places, quantity), f32),
+            pltpu.VMEM((nt, places // nt, quantity), f32),
+            pltpu.VMEM((nt, places // nt, quantity), f32),
+            pltpu.VMEM((places, quantity), f32),
+            pltpu.VMEM((features // LANES, cells, LANES), f32),
+            pltpu.VMEM((2, rows, features), bf16),
+            dma((nt,)),
+            dma((nt,)),
+            dma((2,)),
+            dma((2,)),
+        ],
+        compiler_params=pltpu.CompilerParams(collective_id=2, has_side_effects=True),
+        name="mix_states",
+    )(band, exchange, weights.astype(bf16), latent.reshape(cells, features), driver)
+
+
 def extended(cells, sides, width):
     for axis, dim in sides:
         count = lax.axis_size(axis)
@@ -348,13 +492,6 @@
     return centred * lax.rsqrt(spread + 1e-06) * gain
 
 
-def regrid(flat_fluxes, cell_ids, margin):
-    picked = jnp.take(flat_fluxes, cell_ids, axis=0).astype(jnp.float32)
-    factor = margin.astype(jnp.float32)
-    weighted = jnp.sum(factor[..., None] * picked, axis=0)
-    return (weighted / jnp.sum(factor, axis=0)[..., None]).astype(jnp.bfloat16)
-
-
 def marine_update_kernel(
     marine_present_latent,
     marine_driver_input,
@@ -366,17 +503,14 @@
     pointwise_widen_matrix,
     pointwise_shrink_matrix,
     thermal_projection_matrix,
-    haloed_latent,
     haloed_derivative,
 ):
     horizontal_sum_result, vertical_sum_result, feature_dimension = marine_present_latent.shape
     reach = KS // 2
-    forcing_flat = marine_driver_input.reshape(-1, marine_driver_input.shape[-1])
-    pushed = jnp.dot(
-        forcing_flat, driver_projection_matrix, preferred_element_type=jnp.float32
-    ).reshape(horizontal_sum_result, vertical_sum_result, feature_dimension)
-    mixed = (marine_present_latent.astype(jnp.float32) + pushed).astype(jnp.bfloat16)
-    padded = jnp.pad(haloed_latent(mixed), ((reach, reach), (0, 0), (0, 0))).astype(jnp.float32)
+    forcing_flat, mixed, left, right = marine_driver_input
+    mixed = mixed.reshape(horizontal_sum_result, vertical_sum_result, feature_dimension)
+    haloed = jnp.concatenate([left[:, None], mixed, right[:, None]], axis=1)
+    padded = jnp.pad(haloed, ((reach, reach), (0, 0), (0, 0))).astype(jnp.float32)
     conv_out = jnp.zeros(
         (horizontal_sum_result, vertical_sum_result, feature_dimension), jnp.float32
     )
@@ -481,10 +615,6 @@
     )
 
 
-def pad_state_cols(values):
-    return extended(values, (("tile", 1),), KS // 2)
-
-
 def pad_grad_cols(values):
     return extended(values, (("tile", 1),), KS // 2)
 
@@ -506,13 +636,13 @@
 ):
     band = air_latent_array[0]
     band_rows, band_cols, atmos_width = band.shape
-    fluxes = jnp.dot(
-        band.reshape(-1, atmos_width), air_exchange_projection, preferred_element_type=jnp.float32
-    ).astype(jnp.bfloat16)
-    fluxes = fluxes.reshape(band_rows, band_cols, fluxes.shape[-1])
-    strip = lax.all_to_all(fluxes, "tile", split_axis=1, concat_axis=0, tiled=True)
-    marine_driver_input = regrid(
-        strip.reshape(-1, strip.shape[-1]), intersecting_air_sites, margin_multiplier
+    marine_driver_input = mix_states(
+        band.reshape(-1, atmos_width),
+        air_exchange_projection,
+        intersecting_air_sites,
+        margin_multiplier,
+        marine_latent_array[0],
+        driver_projection_matrix,
     )
     water_indicator_real = terrain_water_indicator.astype(jnp.float32)
     marine_successor_latent, thermal_lowres_field, marine_latent_adjoint, derivative_sequence = (
@@ -527,7 +657,6 @@
             pointwise_widen_matrix,
             pointwise_shrink_matrix,
             thermal_projection_matrix,
-            pad_state_cols,
             pad_grad_cols,
         )
     )

time: 72.7 us -> 71.9 us (0.989)
  Pallas kernels: 32.7 us -> 45.5 us
  starting transfers between devices: 13.6 us -> 3.59 us
  other arithmetic: 7.53 us -> 5.88 us
  waiting for transfers between devices: 1.66 us -> 0.01 us
  local copies, waits for them, and re-layouts: 7.47 us -> 6.7 us
    pallas_call x0 -> x1, Pallas kernels: none -> 13.8 us  [mix_states(): pl.pallas_call(functools.partial(mix_kernel, nt, cols), out_shape=[jax.Sh...]
    all_to_all x1 -> x0, starting transfers between devices: 6.35 us -> none  [body(): lax.all_to_all(fluxes, 'tile', split_axis=1, concat_axis=0, tiled=True)]
    ppermute x2 -> x1, starting transfers between devices: 6.76 us -> 3.53 us  [extended(): lax.ppermute(head, axis, [((i + 1) % count, i) for i in range(count)])]
    gather x1 -> x0, local copies, waits for them, and re-layouts: 3.2 us -> none  [regrid(): picked = jnp.take(flat_fluxes, cell_ids, axis=0).astype(jnp.float32)]
    broadcast_in_dim x1 -> x3, local copies, waits for them, and re-layouts: 0.1 us -> 1.59 us  [the longest x2 1.49 us: marine_update_kernel(): haloed = jnp.concatenate([left[:, None], mixed, right[:, None]], axis=1)]
    ppermute x2 -> x1, waiting for transfers between devices: 1.36 us -> 0.01 us  [extended(): lax.ppermute(tail, axis, [(i, (i + 1) % count) for i in range(count)])]
    dot_general x2 -> x0, matrix products: 1.33 us -> none  [the longest x1 1.1 us: body(): jnp.dot(band.reshape(-1, atmos_width), air_exchange_projection, preferred...]
    unnamed x21 -> x18, local copies, waits for them, and re-layouts: 1 us -> 2.24 us
  transfers between devices with their start and end apart: 5 -> 2, of which waited for: 2 -> 0; matrix products, arithmetic and copies ran while one was open for 10% -> 10% of each run, Pallas kernels for 0% -> 0%
where the time goes in v3:
time: 71.9 us; the launch traced here: 71.3 us
  Pallas kernels  45.5 us (63%)
  matrix products  8.79 us (12%)
  local copies, waits for them, and re-layouts  6.7 us (9%)
  other arithmetic  5.88 us (8%)
  starting transfers between devices  3.59 us (5%)
  between operations  0.84 us (1%)
    pallas_call x1, Pallas kernels, reduce_gradients(): pl.pallas_call(functools.partial(reduce_kernel, scale, ne, nt, rows, plan...  28.7 us
    pallas_call x1, Pallas kernels, mix_states(): pl.pallas_call(functools.partial(mix_kernel, nt, cols), out_shape=[jax.Sh...  13.8 us
    ppermute x1, starting transfers between devices, extended(): lax.ppermute(head, axis, [((i + 1) % count, i) for i in range(count)])  3.53 us
    pallas_call x1, Pallas kernels, reduce_gradients(): pl.pallas_call(functools.partial(unpack_kernel, plan), out_shape=[jax.Sha...  2.97 us
    unnamed x18, local copies, waits for them, and re-layouts  2.24 us
    dot_general x1, matrix products, marine_update_kernel(): jnp.dot(masked_cot, pointwise_shrink_matrix.T, preferred_element_type=jnp...  1.91 us
    dot_general x1, matrix products, marine_update_kernel(): jnp.dot(hidden.T, masked_cot, preferred_element_type=jnp.float32)  1.59 us
    dot_general x1, matrix products, marine_update_kernel(): jnp.dot(hidden, pointwise_shrink_matrix, preferred_element_type=jnp.float32)  1.52 us
  transfers between devices with their start and end apart: 2, of which 0 were waited for; matrix products, arithmetic and copies ran while one was open for 10% of the time, Pallas kernels for 0%

profile of v3, /device:TPU:0, one launch (start us, length us, event | category | flops | bytes accessed | tf_op | source)
XLA Modules:
  0.0 71.3 jit_solution(14950162312062208175)
XLA Ops:
  0.6 0.7 %convert_element_type.59 = f32[32,8]{0,1:T(8,128)S(1)} convert(s32[32,8]{0,1:T(8,128)} %param.24) | non-fusion elementwise | flops 256 | bytes 2048 | tf_op jit(solution)/shard_map/convert_element_type | solution.py:647
  1.4 1.0 %fusion.42 = (f32[1,256]{1,0:T(1,128)S(1)}, f32[1,256]{1,0:T(1,128)S(1)}, f32[1,256]{1,0:T(1,128)S(1)}, f32[1,256]{1,0:T(1,128)S(1)}, f32[1,256]{1,0:T(1,128)S(1...) fusion(f32[9,256]{1,0:T(8,128)} %param.17), kind=kLoop, calls=%fused_computation.83 | loop fusion | bytes 18432 | tf_op jit(solution)/shard_map/slice | solution.py:521
  2.6 0.8 %copy.38 = s32[4,32,8]{2,1,0:T(8,128)S(1)} copy(s32[4,32,8]{1,2,0:T(8,128)} %param.22) | data formatting | bytes 8192 | tf_op args[9]
  3.5 0.8 %copy.39 = s32[4,32,8]{2,1,0:T(8,128)S(1)} copy(s32[4,32,8]{1,2,0:T(8,128)} %param.23) | data formatting | bytes 8192 | tf_op args[10]
  4.4 0.6 convert_element_type.60.weights_ref
  5.0 13.8 %mix_states.1 = (bf16[256,128]{1,0:T(8,128)(2,1)}, bf16[256,256]{1,0:T(8,128)(2,1)}, bf16[32,256]{1,0:T(8,128)(2,1)}, bf16[32,256]{1,0:T(8,128)(2,1)}) custom-call(bf16[16,384]{1,0:T(8,128)(2,1)} %bitcast.83, bf16[384,128]{1,0:T(8,128)(2,1)} %exchange_ref.1, bf16[16,256]{1,0:T(8,128)(2,1)} %convert_element_type.60.weights_ref, bf16[256,256]{1,0:T(8,128)(2,1)} %bitcast.78, ...), custom_call_target="tpu_custom_call" | custom-call | tf_op jit(solution)/shard_map/mix_states/pallas_call | solution.py:446
  18.8 0.7 %copy.41 = bf16[32,1,256]{2,1,0:T(2,128)(2,1)S(1)} copy(bf16[32,1,256]{2,0,1:T(8,128)(2,1)} %bitcast.82) | data formatting | bytes 32768 | tf_op jit(solution)/shard_map/broadcast_in_dim | solution.py:512
  19.5 0.7 %copy.40 = bf16[32,1,256]{2,1,0:T(2,128)(2,1)S(1)} copy(bf16[32,1,256]{2,0,1:T(8,128)(2,1)} %bitcast.81) | data formatting | bytes 32768 | tf_op jit(solution)/shard_map/broadcast_in_dim | solution.py:512
  20.3 1.0 %fusion.10 = f32[34,10,256]{2,1,0:T(8,128)S(1)} fusion(bf16[32,1,256]{2,1,0:T(2,128)(2,1)S(1)} %copy.41, bf16[32,8,256]{2,1,0:T(8,128)(2,1)} %bitcast.80, bf16[32,1,256]{2,1,0:T(2,128)(2,1)S(1)} %copy.40), kind=kLoop, calls=%fused_computation.22 | loop fusion | flops 1044480 | bytes 512000 | tf_op jit(solution)/shard_map/convert_element_type | solution.py:513
  22.0 0.3 fusion.38
  22.5 1.9 %fusion.8 = bf16[256,1024]{1,0:T(8,128)(2,1)S(1)} fusion(f32[256,1024]{1,0:T(8,128)S(1)} %fusion.38, bf16[1024,256]{1,0:T(8,128)(2,1)} %param.20, bf16[1,32,8,256]{3,2,1,0:T(8,128)(2,1)S(1)} %copy-done.4, f32[256]{0:T(256)S(1)} %mul.293), kind=kOutput, calls=%fused_computation.11 | convolution fusion | flops 139657216 | bytes 2229248 | tf_op jit(solution)/shard_map/dot_general | solution.py:566
  24.4 0.9 %multiply_reduce_fusion = (f32[256]{0:T(256)}, f32[256]{0:T(256)S(1)}, f32[256,256]{1,0:T(8,128)S(1)}) fusion(f32[32,8,256]{2,1,0:T(8,128)S(1)} %get-tuple-element.47, f32[256]{0:T(256)S(1)} %rsqrt.10, f32[256]{0:T(256)S(1)} %div.29, f32[256]{0:T(256)S(1)} %copy-done.7, bf16[256,1024]{1,0:T(8,128)(2,1)S(1)} %fusion.8, bf16[256,1024]{1,0:T(8,128)(2,1)S(1)} %copy-done), kind=kOutput, calls=%fused_computation.50 | convolution fusion | flops 134675968 | bytes 1577984 | tf_op jit(solution)/shard_map/dot_general | solution.py:569
  26.0 3.5 %collective-permute-start.1 = (f32[32,1,256]{2,1,0:T(1,128)S(1)}, f32[32,1,256]{2,1,0:T(1,128)S(1)}, u32[]{:S(2)}, u32[]{:S(2)}) collective-permute-start(f32[32,1,256]{2,1,0:T(1,128)S(1)} %get-tuple-element.49), channel_id=1, source_target_pairs={{1,0},{2,1},{3,2},{4,3},{5,4},{6,5},{7,6},{0,7},{9,8},{10,9},{11,1... | collective-permute-start | bytes 98312 | tf_op jit(solution)/shard_map/ppermute | solution.py:482
  29.6 1.5 %fusion.1 = bf16[256,256]{1,0:T(8,128)(2,1)S(1)} fusion(bf16[1024,256]{1,0:T(8,128)(2,1)} %param.20, bf16[256,256]{1,0:T(8,128)(2,1)S(1)} %copy-done.3, f32[256]{0:T(256)S(1)} %mul.293, f32[256,1024]{1,0:T(8,128)S(1)} %fusion.38), kind=kOutput, calls=%fused_computation.4 | convolution fusion | flops 136839168 | bytes 1836032 | tf_op jit(solution)/shard_map/dot_general | solution.py:534
  31.2 1.6 %fusion.30.down_ref = f32[1024,256]{1,0:T(8,128)} fusion(bf16[1,32,8,256]{3,2,1,0:T(8,128)(2,1)S(1)} %copy-done.4, f32[256]{0:T(256)S(1)} %mul.293, f32[256,1024]{1,0:T(8,128)S(1)} %fusion.38), kind=kOutput, calls=%fused_computation.69 | convolution fusion | flops 136773632 | bytes 2229248 | tf_op jit(solution)/shard_map/dot_general | solution.py:565
  32.8 1.5 %fusion.37.up_ref = f32[256,1024]{1,0:T(8,128)} fusion(bf16[256,1024]{1,0:T(8,128)(2,1)S(1)} %fusion.8, f32[32,8,256]{2,1,0:T(8,128)S(1)} %get-tuple-element.47, f32[256]{0:T(256)S(1)} %copy-done.7, f32[256]{0:T(256)S(1)} %rsqrt.10, f32[256]{0:T(256)S(1)} %div.29), kind=kOutput, calls=%fused_computation.78 | convolution fusion | flops 134479872 | bytes 1838080 | tf_op jit(solution)/shard_map/dot_general | solution.py:568
  34.7 0.7 fusion.36.therm_ref
  35.4 1.2 %stack.39.conv_ref = f32[9,256]{1,0:T(8,128)} concatenate(f32[1,256]{1,0:T(1,128)S(1)} %bitcast.109, f32[1,256]{1,0:T(1,128)S(1)} %bitcast.108, f32[1,256]{1,0:T(1,128)S(1)} %bitcast.107, f32[1,256]{1,0:T(1,128)S(1)} %bitcast.106, f32[1,256]{1,0:T(1,128)S(1)} %bitcast.105, f32[1,256]{1,0:T(1,128)S(1)} %bitcast.104, f32[1,256]{1,0:T(1,128)S(1)} %bitcast.103, ...), dimensions={0} | concatenate | bytes 18432 | tf_op jit(solution)/shard_map/stack | solution.py:607
  36.7 0.3 fusion.17
  37.1 0.5 copy-done.6
  37.5 0.9 %fusion.28.force_ref = f32[128,256]{1,0:T(8,128)} fusion(bf16[256,128]{1,0:T(8,128)(2,1)S(1)} %copy-done.6, bf16[32,8,256]{2,1,0:T(8,128)(2,1)S(1)} %fusion.17), kind=kOutput, calls=%fused_computation.65 | convolution fusion | flops 16777216 | bytes 327680 | tf_op jit(solution)/shard_map/dot_general | solution.py:602
  38.4 28.7 %reduce_gradients.1 = (bf16[4608,128]{1,0:T(8,128)(2,1)}, f32[8,2,128]{2,1,0:T(2,128)}) custom-call(f32[256,1024]{1,0:T(8,128)} %fusion.37.up_ref, f32[1024,256]{1,0:T(8,128)} %fusion.30.down_ref, f32[128,256]{1,0:T(8,128)} %fusion.28.force_ref, f32[9,256]{1,0:T(8,128)} %stack.39.conv_ref, f32[1,256]{1,0:T(1,128)} %bitcast.111, f32[8,2,128]{2,1,0:T(2,128)} %fusion.36.therm_ref), custom_call_target="tpu_custom_call" | custom-call | tf_op jit(solution)/shard_map/reduce_gradients/pallas_call | solution.py:284
  67.1 3.0 %unpack_gradients.1 = (bf16[256,1024]{1,0:T(8,128)(2,1)}, bf16[1024,256]{1,0:T(8,128)(2,1)}, bf16[128,256]{1,0:T(8,128)(2,1)}, bf16[9,256]{1,0:T(8,128)(2,1)}, b...) custom-call(bf16[4608,128]{1,0:T(8,128)(2,1)} %get-tuple-element.24.whole, f32[8,2,128]{2,1,0:T(2,128)} %get-tuple-element.25.therm), custom_call_target="tpu_custom_call" | custom-call | tf_op jit(solution)/shard_map/unpack_gradients/pallas_call | solution.py:309
  70.1 1.2 %reduce.2 = bf16[256]{0:T(256)(128)(2,1)} reduce(bf16[1,256]{1,0:T(2,128)(2,1)} %get-tuple-element.29, bf16[]{:T(256)} %constant.37), dimensions={0}, to_apply=%get-tuple-element.29.reduce_sub_computation | reduce | bytes 1026 | tf_op jit(solution)/shard_map/unpack_gradients/pallas_call | solution.py:309
  (42 shorter events, 2.4 us)
Async XLA Ops:
  0.6 21.4 %copy-start = (bf16[256,1024]{1,0:T(8,128)(2,1)S(1)}, bf16[256,1024]{1,0:T(8,128)(2,1)}, u32[]{:S(2)}) copy-start(bf16[256,1024]{1,0:T(8,128)(2,1)} %param.19) | copy-start | bytes 1572868
  21.3 0.7 copy-start.7
  21.6 0.9 %copy-start.4 = (bf16[1,32,8,256]{3,2,1,0:T(8,128)(2,1)S(1)}, bf16[1,32,8,256]{3,2,1,0:T(8,128)(2,1)}, u32[]{:S(2)}) copy-start(bf16[1,32,8,256]{3,2,1,0:T(8,128)(2,1)} %param.25) | copy-start | bytes 393220
  25.6 4.0 %copy-start.3 = (bf16[256,256]{1,0:T(8,128)(2,1)S(1)}, bf16[256,256]{1,0:T(8,128)(2,1)}, u32[]{:S(2)}) copy-start(bf16[256,256]{1,0:T(8,128)(2,1)} %get-tuple-element.20) | copy-start | bytes 393220
  26.0 10.6 %collective-permute-start = (f32[32,1,256]{2,1,0:T(1,128)S(1)}, f32[32,1,256]{2,1,0:T(1,128)S(1)}, u32[]{:S(2)}, u32[]{:S(2)}) collective-permute-start(f32[32,1,256]{2,1,0:T(1,128)S(1)} %get-tuple-element.48), channel_id=1, source_target_pairs={{0,1},{1,2},{2,3},{3,4},{4,5},{5,6},{6,7},{7,0},{8,9},{9,10},{10,1... | collective-permute-start | bytes 98312 | tf_op jit(solution)/shard_map/ppermute | solution.py:480
  26.0 10.5 %collective-permute-start.1 = (f32[32,1,256]{2,1,0:T(1,128)S(1)}, f32[32,1,256]{2,1,0:T(1,128)S(1)}, u32[]{:S(2)}, u32[]{:S(2)}) collective-permute-start(f32[32,1,256]{2,1,0:T(1,128)S(1)} %get-tuple-element.49), channel_id=1, source_target_pairs={{1,0},{2,1},{3,2},{4,3},{5,4},{6,5},{7,6},{0,7},{9,8},{10,9},{11,1... | collective-permute-start | bytes 98312 | tf_op jit(solution)/shard_map/ppermute | solution.py:482
  31.2 3.3 %copy-start.2 = (bf16[256,256]{1,0:T(8,128)(2,1)}, bf16[256,256]{1,0:T(8,128)(2,1)S(1)}, u32[]{:S(2)}) copy-start(bf16[256,256]{1,0:T(8,128)(2,1)S(1)} %fusion.1) | copy-start | bytes 393220
  32.8 1.7 %copy-start.5 = (bf16[256,128]{1,0:T(8,128)(2,1)S(1)}, bf16[256,128]{1,0:T(8,128)(2,1)}, u32[]{:S(2)}) copy-start(bf16[256,128]{1,0:T(8,128)(2,1)} %param.21) | copy-start | bytes 196612
  36.7 0.8 %copy-start.6 = (bf16[256,128]{1,0:T(8,128)(2,1)S(1)}, bf16[256,128]{1,0:T(8,128)(2,1)}, u32[]{:S(2)}) copy-start(bf16[256,128]{1,0:T(8,128)(2,1)} %get-tuple-element.23) | copy-start | bytes 196612
  37.1 30.0 %copy-start.1 = (bf16[32,8,256]{2,1,0:T(8,128)(2,1)}, bf16[32,8,256]{2,1,0:T(8,128)(2,1)S(1)}, u32[]{:S(2)}) copy-start(bf16[32,8,256]{2,1,0:T(8,128)(2,1)S(1)} %fusion.17) | copy-start | bytes 393220

commit v4 on v3

--- a/solution.py
+++ b/solution.py
@@ -259,7 +259,7 @@
         if which == len(outs):
             rows = whole[at : at + count, :].astype(jnp.float32)
             conv_out[:, col : col + LANES] = rows[:taps].astype(jnp.bfloat16)
-            gain_out[:, col : col + LANES] = rows[taps : taps + 1].astype(jnp.bfloat16)
+            gain_out[col : col + LANES] = rows[taps].astype(jnp.bfloat16)
     tiles, columns, _ = therm.shape
     for t in range(tiles):
         strip[t * columns : (t + 1) * columns, :] = therm[t]
@@ -313,7 +313,7 @@
             jax.ShapeDtypeStruct(down.shape, bf16),
             jax.ShapeDtypeStruct(force.shape, bf16),
             jax.ShapeDtypeStruct(conv.shape, bf16),
-            jax.ShapeDtypeStruct(gain.shape, bf16),
+            jax.ShapeDtypeStruct((features,), bf16),
             jax.ShapeDtypeStruct((1, tiles * columns, quantity), bf16),
         ],
         in_specs=[vmem] * 2,
@@ -336,14 +336,13 @@
     driver_ref,
     forcing_out,
     mixed_out,
-    left_out,
-    right_out,
+    padded,
     flux,
     slabs,
     strip_in,
     strip,
-    state,
     edges,
+    halo,
     s_send,
     s_recv,
     h_send,
@@ -401,21 +400,16 @@
         latent_ref[...].astype(f32)
         + jnp.dot(forcing, driver_ref[...], preferred_element_type=f32)
     ).astype(bf16)
-    for lane in range(0, mixed.shape[1], LANES):
-        state[lane // LANES] = mixed[:, lane : lane + LANES].astype(f32)
-    rows = edges.shape[1]
-    for side, column in ((0, cols - 1), (1, 0)):
-        for lane in range(0, mixed.shape[1], LANES):
-            edges[side, :, lane : lane + LANES] = state[
-                lane // LANES, pl.ds(column, rows, stride=cols), :
-            ].astype(bf16)
-    hops = ((0, left_out, (tile + 1) % nt), (1, right_out, (tile + nt - 1) % nt))
+    cube = mixed.astype(f32).reshape(edges.shape[1], cols, mixed.shape[1])
+    edges[0] = cube[:, cols - 1 : cols, :]
+    edges[1] = cube[:, 0:1, :]
+    hops = ((0, (tile + 1) % nt), (1, (tile + nt - 1) % nt))
     halos = []
-    for side, out, to in hops:
+    for side, to in hops:
         halos.append(
             pltpu.make_async_remote_copy(
                 src_ref=edges.at[side],
-                dst_ref=out,
+                dst_ref=halo.at[side],
                 send_sem=h_send.at[side],
                 recv_sem=h_recv.at[side],
                 device_id={"tile": to},
@@ -424,8 +418,14 @@
         )
         halos[-1].start()
     mixed_out[...] = mixed
+    rows = edges.shape[1]
+    padded[0] = jnp.zeros_like(padded[0])
+    padded[rows + 1] = jnp.zeros_like(padded[0])
+    padded[1 : rows + 1, 1 : cols + 1, :] = cube
     for copy in halos:
         copy.wait_recv()
+    padded[1 : rows + 1, 0:1, :] = halo[0]
+    padded[1 : rows + 1, cols + 1 : cols + 2, :] = halo[1]
     for copy in copies + halos:
         copy.wait_send()
 
@@ -436,8 +436,8 @@
     quantity = exchange.shape[1]
     places = band.shape[0]
     cells = rows * cols
-    flat_sites = sites.reshape(sites.shape[0], 1, cells)
-    flat_margin = margin.reshape(margin.shape[0], 1, cells)
+    both = (margin * places + sites).reshape(sites.shape[0], 1, cells)
+    flat_sites, flat_margin = both % places, both // places
     names = lax.broadcasted_iota(jnp.int32, (1, places, 1), 1)
     weights = jnp.sum(jnp.where(flat_sites == names, flat_margin, 0), axis=0)
     bf16, f32 = jnp.bfloat16, jnp.float32
@@ -448,18 +448,17 @@
         out_shape=[
             jax.ShapeDtypeStruct((cells, quantity), bf16),
             jax.ShapeDtypeStruct((cells, features), bf16),
-            jax.ShapeDtypeStruct((rows, features), bf16),
-            jax.ShapeDtypeStruct((rows, features), bf16),
+            jax.ShapeDtypeStruct((rows + 2, cols + 2, features), f32),
         ],
         in_specs=[vmem] * 5,
-        out_specs=[vmem] * 4,
+        out_specs=[vmem] * 3,
         scratch_shapes=[
             pltpu.VMEM((places, quantity), f32),
             pltpu.VMEM((nt, places // nt, quantity), f32),
             pltpu.VMEM((nt, places // nt, quantity), f32),
             pltpu.VMEM((places, quantity), f32),
-            pltpu.VMEM((features // LANES, cells, LANES), f32),
-            pltpu.VMEM((2, rows, features), bf16),
+            pltpu.VMEM((2, rows, 1, features), f32),
+            pltpu.VMEM((2, rows, 1, features), f32),
             dma((nt,)),
             dma((nt,)),
             dma((2,)),
@@ -507,10 +506,8 @@
 ):
     horizontal_sum_result, vertical_sum_result, feature_dimension = marine_present_latent.shape
     reach = KS // 2
-    forcing_flat, mixed, left, right = marine_driver_input
+    forcing_flat, mixed, padded = marine_driver_input
     mixed = mixed.reshape(horizontal_sum_result, vertical_sum_result, feature_dimension)
-    haloed = jnp.concatenate([left[:, None], mixed, right[:, None]], axis=1)
-    padded = jnp.pad(haloed, ((reach, reach), (0, 0), (0, 0))).astype(jnp.float32)
     conv_out = jnp.zeros(
         (horizontal_sum_result, vertical_sum_result, feature_dimension), jnp.float32
     )
@@ -683,7 +680,7 @@
         marine_latent_adjoint[None],
         force,
         conv,
-        gain.reshape(-1),
+        gain,
         up,
         down,
     )

time: 71.9 us -> 69.3 us (0.964)
  local copies, waits for them, and re-layouts: 6.7 us -> 3.79 us
  other arithmetic: 5.88 us -> 7.1 us
  matrix products: 8.79 us -> 7.66 us
    reduce_sum x2, other arithmetic: 0.53 us -> 3.22 us  [layer_norm(): centred = values - jnp.mean(values, axis=-1, keepdims=True)]
    broadcast_in_dim x3 -> x0, local copies, waits for them, and re-layouts: 1.59 us -> none  [the longest x2 1.49 us: marine_update_kernel(): haloed = jnp.concatenate([left[:, None], mixed, right[:, None]], axis=1)]
    unnamed x18, local copies, waits for them, and re-layouts: 2.24 us -> 0.84 us
    pallas_call x1 -> x0, other arithmetic: 1.19 us -> none  [reduce_gradients(): pl.pallas_call(functools.partial(unpack_kernel, plan), out_shape=[jax.Sha...]
    dot_general x1, matrix products: 1.91 us -> 0.87 us  [marine_update_kernel(): jnp.dot(masked_cot, pointwise_shrink_matrix.T, preferred_element_type=jnp...]
    convert_element_type x1 -> x0, other arithmetic: 1.03 us -> none  [marine_update_kernel(): jnp.pad(haloed, ((reach, reach), (0, 0), (0, 0))).astype(jnp.float32)]
    add x0 -> x1, other arithmetic: none -> 0.74 us  [mix_states(): both = (margin * places + sites).reshape(sites.shape[0], 1, cells)]
where the time goes in v4:
time: 69.3 us; the launch traced here: 68.9 us
  Pallas kernels  45.9 us (66%)
  matrix products  7.66 us (11%)
  other arithmetic  7.1 us (10%)
  local copies, waits for them, and re-layouts  3.79 us (5%)
  starting transfers between devices  3.59 us (5%)
  between operations  0.86 us (1%)
    pallas_call x1, Pallas kernels, reduce_gradients(): pl.pallas_call(functools.partial(reduce_kernel, scale, ne, nt, rows, plan...  28.7 us
    pallas_call x1, Pallas kernels, mix_states(): pl.pallas_call(functools.partial(mix_kernel, nt, cols), out_shape=[jax.Sh...  14.2 us
    ppermute x1, starting transfers between devices, extended(): lax.ppermute(head, axis, [((i + 1) % count, i) for i in range(count)])  3.53 us
    reduce_sum x2, other arithmetic, layer_norm(): centred = values - jnp.mean(values, axis=-1, keepdims=True)  3.22 us
    pallas_call x1, Pallas kernels, reduce_gradients(): pl.pallas_call(functools.partial(unpack_kernel, plan), out_shape=[jax.Sha...  2.97 us
    dot_general x1, matrix products, marine_update_kernel(): jnp.dot(hidden.T, masked_cot, preferred_element_type=jnp.float32)  1.6 us
    dot_general x1, matrix products, marine_update_kernel(): grad_up = jnp.dot(normed.T, pre_cot, preferred_element_type=jnp.float32)  1.48 us
    dot_general x1, matrix products, marine_update_kernel(): jnp.dot(hidden, pointwise_shrink_matrix, preferred_element_type=jnp.float32)  1.41 us
  transfers between devices with their start and end apart: 2, of which 0 were waited for; matrix products, arithmetic and copies ran while one was open for 10% of the time, Pallas kernels for 0%

profile of v4, /device:TPU:0, one launch (start us, length us, event | category | flops | bytes accessed | tf_op | source)
XLA Modules:
  0.0 68.9 jit_solution(3581876535157206917)
XLA Ops:
  0.6 0.7 %convert_element_type.54 = f32[32,8]{0,1:T(8,128)S(1)} convert(s32[32,8]{0,1:T(8,128)} %param.24) | non-fusion elementwise | flops 256 | bytes 2048 | tf_op jit(solution)/shard_map/convert_element_type | solution.py:644
  1.4 1.0 %fusion.41 = (f32[1,256]{1,0:T(1,128)S(1)}, f32[1,256]{1,0:T(1,128)S(1)}, f32[1,256]{1,0:T(1,128)S(1)}, f32[1,256]{1,0:T(1,128)S(1)}, f32[1,256]{1,0:T(1,128)S(1...) fusion(f32[9,256]{1,0:T(8,128)} %param.17), kind=kLoop, calls=%fused_computation.88 | loop fusion | bytes 18432 | tf_op jit(solution)/shard_map/slice | solution.py:518
  2.6 0.7 %multiply_add_fusion.2 = s32[4,32,8]{1,2,0:T(8,128)S(1)} fusion(s32[4,32,8]{1,2,0:T(8,128)} %param.22, s32[4,32,8]{1,2,0:T(8,128)} %param.23), kind=kLoop, calls=%fused_computation.68 | loop fusion | flops 2048 | bytes 12288 | tf_op jit(solution)/shard_map/add | solution.py:439
  3.5 0.6 convert_element_type.55.weights_ref
  4.1 14.2 %mix_states.1 = (bf16[256,128]{1,0:T(8,128)(2,1)}, bf16[256,256]{1,0:T(8,128)(2,1)}, f32[34,10,256]{2,1,0:T(8,128)}) custom-call(bf16[16,384]{1,0:T(8,128)(2,1)} %bitcast.77, bf16[384,128]{1,0:T(8,128)(2,1)} %exchange_ref.1, bf16[16,256]{1,0:T(8,128)(2,1)} %convert_element_type.55.weights_ref, bf16[256,256]{1,0:T(8,128)(2,1)} %bitcast.75, ...), custom_call_target="tpu_custom_call" | custom-call | tf_op jit(solution)/shard_map/mix_states/pallas_call | solution.py:446
  18.4 3.0 %fusion.39 = (f32[32,8]{1,0:T(8,128)S(1)}, f32[32,8,256]{2,1,0:T(8,128)S(1)}) fusion(f32[34,10,256]{2,1,0:T(8,128)} %get-tuple-element.20, f32[256]{0:T(256)S(1)} %bitcast.92, f32[256]{0:T(256)S(1)} %bitcast.94, f32[256]{0:T(256)S(1)} %bitcast.80, f32[256]{0:T(256)S(1)} %bitcast.82, f32[256]{0:T(256)S(1)} %bitcast.84, f32[256]{0:T(256)S(1)} %bitcast.86, ...), kind=kLoop, calls=%fused_computation.86 | loop fusion | flops 1179392 | bytes 2631680 | tf_op jit(solution)/shard_map/jvp()/reduce_sum | solution.py:489
  21.4 0.2 multiply_reduce_fusion.11
  21.7 0.3 fusion.37
  22.2 0.2 copy-done.8
  22.4 0.9 %fusion.8 = bf16[256,1024]{1,0:T(8,128)(2,1)S(1)} fusion(f32[256,1024]{1,0:T(8,128)S(1)} %fusion.37, bf16[1024,256]{1,0:T(8,128)(2,1)S(1)} %copy-done.8, bf16[1,32,8,256]{3,2,1,0:T(8,128)(2,1)S(1)} %copy-done.4, f32[256]{0:T(256)S(1)} %mul.299), kind=kOutput, calls=%fused_computation.11 | convolution fusion | flops 139657216 | bytes 2229248 | tf_op jit(solution)/shard_map/dot_general | solution.py:563
  23.3 0.9 %multiply_reduce_fusion = (f32[256]{0:T(256)}, f32[256]{0:T(256)S(1)}, f32[256,256]{1,0:T(8,128)S(1)}) fusion(f32[32,8,256]{2,1,0:T(8,128)S(1)} %get-tuple-element.45, f32[256]{0:T(256)S(1)} %rsqrt.10, f32[256]{0:T(256)S(1)} %div.45, f32[256]{0:T(256)S(1)} %copy-done.7, bf16[256,1024]{1,0:T(8,128)(2,1)S(1)} %fusion.8, bf16[256,1024]{1,0:T(8,128)(2,1)S(1)} %copy-done), kind=kOutput, calls=%fused_computation.46 | convolution fusion | flops 134675968 | bytes 1577984 | tf_op jit(solution)/shard_map/dot_general | solution.py:566
  24.3 0.3 fusion.38
  24.5 0.3 multiply_reduce_fusion.1
  24.9 3.5 %collective-permute-start.1 = (f32[32,1,256]{2,1,0:T(1,128)S(1)}, f32[32,1,256]{2,1,0:T(1,128)S(1)}, u32[]{:S(2)}, u32[]{:S(2)}) collective-permute-start(f32[32,1,256]{2,1,0:T(1,128)S(1)} %get-tuple-element.47), channel_id=1, source_target_pairs={{1,0},{2,1},{3,2},{4,3},{5,4},{6,5},{7,6},{0,7},{9,8},{10,9},{11,1... | collective-permute-start | bytes 98312 | tf_op jit(solution)/shard_map/ppermute | solution.py:481
  28.5 1.6 %fusion.28.down_ref = f32[1024,256]{1,0:T(8,128)} fusion(bf16[1,32,8,256]{3,2,1,0:T(8,128)(2,1)S(1)} %copy-done.4, f32[256]{0:T(256)S(1)} %mul.299, f32[256,1024]{1,0:T(8,128)S(1)} %fusion.37), kind=kOutput, calls=%fused_computation.65 | convolution fusion | flops 136773632 | bytes 2229248 | tf_op jit(solution)/shard_map/dot_general | solution.py:562
  30.1 1.5 %fusion.36.up_ref = f32[256,1024]{1,0:T(8,128)} fusion(bf16[256,1024]{1,0:T(8,128)(2,1)S(1)} %fusion.8, f32[32,8,256]{2,1,0:T(8,128)S(1)} %get-tuple-element.45, f32[256]{0:T(256)S(1)} %copy-done.7, f32[256]{0:T(256)S(1)} %rsqrt.10, f32[256]{0:T(256)S(1)} %div.45), kind=kOutput, calls=%fused_computation.83 | convolution fusion | flops 134479872 | bytes 1838080 | tf_op jit(solution)/shard_map/dot_general | solution.py:565
  31.8 1.4 %fusion.1 = bf16[256,256]{1,0:T(8,128)(2,1)S(1)} fusion(bf16[1024,256]{1,0:T(8,128)(2,1)S(1)} %copy-done.8, bf16[256,256]{1,0:T(8,128)(2,1)} %get-tuple-element.19, f32[256]{0:T(256)S(1)} %mul.299, f32[256,1024]{1,0:T(8,128)S(1)} %fusion.37), kind=kOutput, calls=%fused_computation.4 | convolution fusion | flops 136839168 | bytes 1836032 | tf_op jit(solution)/shard_map/dot_general | solution.py:531
  33.5 0.7 fusion.34.therm_ref
  34.2 1.2 %stack.39.conv_ref = f32[9,256]{1,0:T(8,128)} concatenate(f32[1,256]{1,0:T(1,128)S(1)} %bitcast.103, f32[1,256]{1,0:T(1,128)S(1)} %bitcast.102, f32[1,256]{1,0:T(1,128)S(1)} %bitcast.101, f32[1,256]{1,0:T(1,128)S(1)} %bitcast.100, f32[1,256]{1,0:T(1,128)S(1)} %bitcast.99, f32[1,256]{1,0:T(1,128)S(1)} %bitcast.98, f32[1,256]{1,0:T(1,128)S(1)} %bitcast.97, f32[1,256]{1,0:T(1,128)S(1)} %bitcast.104, ...), dimensions={0} | concatenate | bytes 18432 | tf_op jit(solution)/shard_map/stack | solution.py:604
  35.5 0.4 fusion.15
  35.9 0.5 copy-done.6
  36.3 0.9 %fusion.26.force_ref = f32[128,256]{1,0:T(8,128)} fusion(bf16[256,128]{1,0:T(8,128)(2,1)S(1)} %copy-done.6, bf16[32,8,256]{2,1,0:T(8,128)(2,1)S(1)} %fusion.15), kind=kOutput, calls=%fused_computation.61 | convolution fusion | flops 16777216 | bytes 327680 | tf_op jit(solution)/shard_map/dot_general | solution.py:599
  37.2 28.7 %reduce_gradients.1 = (bf16[4608,128]{1,0:T(8,128)(2,1)}, f32[8,2,128]{2,1,0:T(2,128)}) custom-call(f32[256,1024]{1,0:T(8,128)} %fusion.36.up_ref, f32[1024,256]{1,0:T(8,128)} %fusion.28.down_ref, f32[128,256]{1,0:T(8,128)} %fusion.26.force_ref, f32[9,256]{1,0:T(8,128)} %stack.39.conv_ref, f32[1,256]{1,0:T(1,128)} %bitcast.105, f32[8,2,128]{2,1,0:T(2,128)} %fusion.34.therm_ref), custom_call_target="tpu_custom_call" | custom-call | tf_op jit(solution)/shard_map/reduce_gradients/pallas_call | solution.py:284
  65.9 3.0 %unpack_gradients.1 = (bf16[256,1024]{1,0:T(8,128)(2,1)}, bf16[1024,256]{1,0:T(8,128)(2,1)}, bf16[128,256]{1,0:T(8,128)(2,1)}, bf16[9,256]{1,0:T(8,128)(2,1)}, b...) custom-call(bf16[4608,128]{1,0:T(8,128)(2,1)} %get-tuple-element.22.whole, f32[8,2,128]{2,1,0:T(2,128)} %get-tuple-element.23.therm), custom_call_target="tpu_custom_call" | custom-call | tf_op jit(solution)/shard_map/unpack_gradients/pallas_call | solution.py:309
  (40 shorter events, 1.4 us)
Async XLA Ops:
  0.6 21.1 %copy-start = (bf16[256,1024]{1,0:T(8,128)(2,1)S(1)}, bf16[256,1024]{1,0:T(8,128)(2,1)}, u32[]{:S(2)}) copy-start(bf16[256,1024]{1,0:T(8,128)(2,1)} %param.19) | copy-start | bytes 1572868
  18.4 3.4 %copy-start.7 = (f32[256]{0:T(256)S(1)}, f32[256]{0:T(256)}, u32[]{:S(2)}) copy-start(f32[256]{0:T(256)} %param.18) | copy-start | bytes 3076
  21.3 0.9 %copy-start.4 = (bf16[1,32,8,256]{3,2,1,0:T(8,128)(2,1)S(1)}, bf16[1,32,8,256]{3,2,1,0:T(8,128)(2,1)}, u32[]{:S(2)}) copy-start(bf16[1,32,8,256]{3,2,1,0:T(8,128)(2,1)} %param.25) | copy-start | bytes 393220
  21.3 1.1 %copy-start.8 = (bf16[1024,256]{1,0:T(8,128)(2,1)S(1)}, bf16[1024,256]{1,0:T(8,128)(2,1)}, u32[]{:S(2)}) copy-start(bf16[1024,256]{1,0:T(8,128)(2,1)} %param.20) | copy-start | bytes 1572868
  23.3 1.2 %copy-start.1 = (f32[34,10,256]{2,1,0:T(8,128)S(1)}, f32[34,10,256]{2,1,0:T(8,128)}, u32[]{:S(2)}) copy-start(f32[34,10,256]{2,1,0:T(8,128)} %get-tuple-element.20) | copy-start | bytes 1044484
  24.9 10.5 %collective-permute-start = (f32[32,1,256]{2,1,0:T(1,128)S(1)}, f32[32,1,256]{2,1,0:T(1,128)S(1)}, u32[]{:S(2)}, u32[]{:S(2)}) collective-permute-start(f32[32,1,256]{2,1,0:T(1,128)S(1)} %get-tuple-element.46), channel_id=1, source_target_pairs={{0,1},{1,2},{2,3},{3,4},{4,5},{5,6},{6,7},{7,0},{8,9},{9,10},{10,1... | collective-permute-start | bytes 98312 | tf_op jit(solution)/shard_map/ppermute | solution.py:479
  24.9 10.4 %collective-permute-start.1 = (f32[32,1,256]{2,1,0:T(1,128)S(1)}, f32[32,1,256]{2,1,0:T(1,128)S(1)}, u32[]{:S(2)}, u32[]{:S(2)}) collective-permute-start(f32[32,1,256]{2,1,0:T(1,128)S(1)} %get-tuple-element.47), channel_id=1, source_target_pairs={{1,0},{2,1},{3,2},{4,3},{5,4},{6,5},{7,6},{0,7},{9,8},{10,9},{11,1... | collective-permute-start | bytes 98312 | tf_op jit(solution)/shard_map/ppermute | solution.py:481
  31.8 1.4 %copy-start.5 = (bf16[256,128]{1,0:T(8,128)(2,1)S(1)}, bf16[256,128]{1,0:T(8,128)(2,1)}, u32[]{:S(2)}) copy-start(bf16[256,128]{1,0:T(8,128)(2,1)} %param.21) | copy-start | bytes 196612
  33.2 2.6 %copy-start.3 = (bf16[256,256]{1,0:T(8,128)(2,1)}, bf16[256,256]{1,0:T(8,128)(2,1)S(1)}, u32[]{:S(2)}) copy-start(bf16[256,256]{1,0:T(8,128)(2,1)S(1)} %fusion.1) | copy-start | bytes 393220
  35.5 0.8 %copy-start.6 = (bf16[256,128]{1,0:T(8,128)(2,1)S(1)}, bf16[256,128]{1,0:T(8,128)(2,1)}, u32[]{:S(2)}) copy-start(bf16[256,128]{1,0:T(8,128)(2,1)} %get-tuple-element.21) | copy-start | bytes 196612
  35.9 30.0 %copy-start.2 = (bf16[32,8,256]{2,1,0:T(8,128)(2,1)}, bf16[32,8,256]{2,1,0:T(8,128)(2,1)S(1)}, u32[]{:S(2)}) copy-start(bf16[32,8,256]{2,1,0:T(8,128)(2,1)S(1)} %fusion.15) | copy-start | bytes 393220

commit v5 on v4

--- a/solution.py
+++ b/solution.py
@@ -100,9 +100,10 @@
             barrier, inc=1, device_id={"ens": (ens + o) % ne}, device_id_type=MESH
         )
 
-    taps = conv_ref.shape[0]
+    taps = len(conv_ref)
     small[...] = jnp.zeros_like(small)
-    small[0:taps, :] = conv_ref[...]
+    for tap in range(taps):
+        small[tap : tap + 1, :] = conv_ref[tap][...]
     small[taps : taps + 1, :] = gain_ref[...]
     ins = (up_ref, down_ref, force_ref, small)
     if used < SLABS * slab:
@@ -271,7 +272,7 @@
 def reduce_gradients(up, down, force, conv, gain, therm, scale):
     ne, nt = lax.axis_size("ens"), lax.axis_size("tile")
     nz = nt // 2
-    taps, features = conv.shape
+    taps, features = len(conv), conv[0].shape[1]
     small_rows = -(-(taps + 1) // 16) * 16
     plan, used = pack_plan([up.shape, down.shape, force.shape, (small_rows, features)])
     rows = -(-used // (SLABS * 2 * ne * nz * 16)) * 16
@@ -287,7 +288,7 @@
             jax.ShapeDtypeStruct((SLABS * 2 * ne * block, LANES), bf16),
             jax.ShapeDtypeStruct(therm.shape, therm.dtype),
         ],
-        in_specs=[vmem] * 6,
+        in_specs=[vmem] * 3 + [[vmem] * taps] + [vmem] * 2,
         out_specs=[vmem] * 2,
         scratch_shapes=[
             pltpu.VMEM((small_rows, features), jnp.float32),
@@ -312,7 +313,7 @@
             jax.ShapeDtypeStruct(up.shape, bf16),
             jax.ShapeDtypeStruct(down.shape, bf16),
             jax.ShapeDtypeStruct(force.shape, bf16),
-            jax.ShapeDtypeStruct(conv.shape, bf16),
+            jax.ShapeDtypeStruct((taps, features), bf16),
             jax.ShapeDtypeStruct((features,), bf16),
             jax.ShapeDtypeStruct((1, tiles * columns, quantity), bf16),
         ],
@@ -601,7 +602,7 @@
         marine_latent_adjoint.reshape(-1, feature_dimension),
         preferred_element_type=jnp.float32,
     )
-    derivative_sequence = (grad_force, jnp.stack(tap_grads), grad_gain, grad_up, grad_down)
+    derivative_sequence = (grad_force, [values.reshape(1, -1) for values in tap_grads], grad_gain, grad_up, grad_down)
     return (
         marine_successor_latent.reshape(
             horizontal_sum_result, vertical_sum_result, feature_dimension

time: 69.3 us -> 68.8 us (level)
  local copies, waits for them, and re-layouts: 3.79 us -> 2.55 us
    another operation x1 -> x0, local copies, waits for them, and re-layouts: 1.23 us -> none  [marine_update_kernel(): jnp.stack(tap_grads)]
  transfers between devices with their start and end apart: 2 -> 2, of which waited for: 0 -> 0; matrix products, arithmetic and copies ran while one was open for 10% -> 8% of each run, Pallas kernels for 0% -> 0%
where the time goes in v5:
time: 68.8 us; the launch traced here: 68.3 us
  Pallas kernels  45.9 us (67%)
  other arithmetic  7.74 us (11%)
  matrix products  7.66 us (11%)
  starting transfers between devices  3.59 us (5%)
  local copies, waits for them, and re-layouts  2.55 us (4%)
  between operations  0.85 us (1%)
    pallas_call x1, Pallas kernels, reduce_gradients(): pl.pallas_call(functools.partial(reduce_kernel, scale, ne, nt, rows, plan...  28.8 us
    pallas_call x1, Pallas kernels, mix_states(): pl.pallas_call(functools.partial(mix_kernel, nt, cols), out_shape=[jax.Sh...  14.2 us
    ppermute x1, starting transfers between devices, extended(): lax.ppermute(head, axis, [((i + 1) % count, i) for i in range(count)])  3.53 us
    reduce_sum x2, other arithmetic, layer_norm(): centred = values - jnp.mean(values, axis=-1, keepdims=True)  3.23 us
    pallas_call x1, Pallas kernels, reduce_gradients(): pl.pallas_call(functools.partial(unpack_kernel, plan), out_shape=[jax.Sha...  2.97 us
    dot_general x1, matrix products, marine_update_kernel(): jnp.dot(hidden.T, masked_cot, preferred_element_type=jnp.float32)  1.6 us
    dot_general x1, matrix products, marine_update_kernel(): grad_up = jnp.dot(normed.T, pre_cot, preferred_element_type=jnp.float32)  1.48 us
    dot_general x1, matrix products, marine_update_kernel(): jnp.dot(hidden, pointwise_shrink_matrix, preferred_element_type=jnp.float32)  1.41 us
  transfers between devices with their start and end apart: 2, of which 0 were waited for; matrix products, arithmetic and copies ran while one was open for 8% of the time, Pallas kernels for 0%

profile of v5, /device:TPU:0, one launch (start us, length us, event | category | flops | bytes accessed | tf_op | source)
XLA Modules:
  0.0 68.3 jit_solution(8530443169236813744)
XLA Ops:
  0.6 0.7 %convert_element_type.54 = f32[32,8]{0,1:T(8,128)S(1)} convert(s32[32,8]{0,1:T(8,128)} %param.24) | non-fusion elementwise | flops 256 | bytes 2048 | tf_op jit(solution)/shard_map/convert_element_type | solution.py:645
  1.4 1.0 %fusion.41 = (f32[1,256]{1,0:T(1,128)S(1)}, f32[1,256]{1,0:T(1,128)S(1)}, f32[1,256]{1,0:T(1,128)S(1)}, f32[1,256]{1,0:T(1,128)S(1)}, f32[1,256]{1,0:T(1,128)S(1...) fusion(f32[9,256]{1,0:T(8,128)} %param.17), kind=kLoop, calls=%fused_computation.88 | loop fusion | bytes 18432 | tf_op jit(solution)/shard_map/slice | solution.py:519
  2.6 0.7 %multiply_add_fusion.2 = s32[4,32,8]{1,2,0:T(8,128)S(1)} fusion(s32[4,32,8]{1,2,0:T(8,128)} %param.22, s32[4,32,8]{1,2,0:T(8,128)} %param.23), kind=kLoop, calls=%fused_computation.68 | loop fusion | flops 2048 | bytes 12288 | tf_op jit(solution)/shard_map/add | solution.py:440
  3.5 0.6 convert_element_type.55.weights_ref
  4.1 14.2 %mix_states.1 = (bf16[256,128]{1,0:T(8,128)(2,1)}, bf16[256,256]{1,0:T(8,128)(2,1)}, f32[34,10,256]{2,1,0:T(8,128)}) custom-call(bf16[16,384]{1,0:T(8,128)(2,1)} %bitcast.77, bf16[384,128]{1,0:T(8,128)(2,1)} %exchange_ref.1, bf16[16,256]{1,0:T(8,128)(2,1)} %convert_element_type.55.weights_ref, bf16[256,256]{1,0:T(8,128)(2,1)} %bitcast.75, ...), custom_call_target="tpu_custom_call" | custom-call | tf_op jit(solution)/shard_map/mix_states/pallas_call | solution.py:447
  18.4 3.0 %fusion.39 = (f32[32,8]{1,0:T(8,128)S(1)}, f32[32,8,256]{2,1,0:T(8,128)S(1)}) fusion(f32[34,10,256]{2,1,0:T(8,128)} %get-tuple-element.20, f32[256]{0:T(256)S(1)} %bitcast.92, f32[256]{0:T(256)S(1)} %bitcast.94, f32[256]{0:T(256)S(1)} %bitcast.80, f32[256]{0:T(256)S(1)} %bitcast.82, f32[256]{0:T(256)S(1)} %bitcast.84, f32[256]{0:T(256)S(1)} %bitcast.86, ...), kind=kLoop, calls=%fused_computation.86 | loop fusion | flops 1179392 | bytes 2631680 | tf_op jit(solution)/shard_map/jvp()/reduce_sum | solution.py:490
  21.4 0.2 multiply_reduce_fusion.11
  21.7 0.4 fusion.37
  22.2 0.2 copy-done.8
  22.4 0.9 %fusion.8 = bf16[256,1024]{1,0:T(8,128)(2,1)S(1)} fusion(f32[256,1024]{1,0:T(8,128)S(1)} %fusion.37, bf16[1024,256]{1,0:T(8,128)(2,1)S(1)} %copy-done.8, bf16[1,32,8,256]{3,2,1,0:T(8,128)(2,1)S(1)} %copy-done.4, f32[256]{0:T(256)S(1)} %mul.299), kind=kOutput, calls=%fused_computation.11 | convolution fusion | flops 139657216 | bytes 2229248 | tf_op jit(solution)/shard_map/dot_general | solution.py:564
  23.3 0.9 %multiply_reduce_fusion = (f32[256]{0:T(256)}, f32[256]{0:T(256)S(1)}, f32[256,256]{1,0:T(8,128)S(1)}) fusion(f32[32,8,256]{2,1,0:T(8,128)S(1)} %get-tuple-element.45, f32[256]{0:T(256)S(1)} %rsqrt.10, f32[256]{0:T(256)S(1)} %div.45, f32[256]{0:T(256)S(1)} %copy-done.7, bf16[256,1024]{1,0:T(8,128)(2,1)S(1)} %fusion.8, bf16[256,1024]{1,0:T(8,128)(2,1)S(1)} %copy-done), kind=kOutput, calls=%fused_computation.46 | convolution fusion | flops 134675968 | bytes 1577984 | tf_op jit(solution)/shard_map/dot_general | solution.py:567
  24.3 0.3 fusion.38
  24.5 0.9 %multiply_reduce_fusion.1 = (f32[256]{0:T(256)}, f32[256]{0:T(256)}, f32[256]{0:T(256)}, f32[256]{0:T(256)}, f32[256]{0:T(256)}, /*index=5*/f32[256]{0:T(256)}, ...) fusion(f32[34,10,256]{2,1,0:T(8,128)S(1)} %copy-done.1, f32[256,256]{1,0:T(8,128)S(1)} %get-tuple-element.43, ...), kind=kLoop, calls=%fused_computation.47 | loop fusion | flops 1242880 | bytes 2893824 | tf_op jit(solution)/shard_map/reduce_sum | solution.py:574
  25.6 3.5 %collective-permute-start.1 = (f32[32,1,256]{2,1,0:T(1,128)S(1)}, f32[32,1,256]{2,1,0:T(1,128)S(1)}, u32[]{:S(2)}, u32[]{:S(2)}) collective-permute-start(f32[32,1,256]{2,1,0:T(1,128)S(1)} %get-tuple-element.47), channel_id=1, source_target_pairs={{1,0},{2,1},{3,2},{4,3},{5,4},{6,5},{7,6},{0,7},{9,8},{10,9},{11,1... | collective-permute-start | bytes 98312 | tf_op jit(solution)/shard_map/ppermute | solution.py:482
  29.2 1.6 %fusion.28.down_ref = f32[1024,256]{1,0:T(8,128)} fusion(bf16[1,32,8,256]{3,2,1,0:T(8,128)(2,1)S(1)} %copy-done.4, f32[256]{0:T(256)S(1)} %mul.299, f32[256,1024]{1,0:T(8,128)S(1)} %fusion.37), kind=kOutput, calls=%fused_computation.65 | convolution fusion | flops 136773632 | bytes 2229248 | tf_op jit(solution)/shard_map/dot_general | solution.py:563
  30.8 1.5 %fusion.36.up_ref = f32[256,1024]{1,0:T(8,128)} fusion(bf16[256,1024]{1,0:T(8,128)(2,1)S(1)} %fusion.8, f32[32,8,256]{2,1,0:T(8,128)S(1)} %get-tuple-element.45, f32[256]{0:T(256)S(1)} %copy-done.7, f32[256]{0:T(256)S(1)} %rsqrt.10, f32[256]{0:T(256)S(1)} %div.45), kind=kOutput, calls=%fused_computation.83 | convolution fusion | flops 134479872 | bytes 1838080 | tf_op jit(solution)/shard_map/dot_general | solution.py:566
  32.4 1.4 %fusion.1 = bf16[256,256]{1,0:T(8,128)(2,1)S(1)} fusion(bf16[1024,256]{1,0:T(8,128)(2,1)S(1)} %copy-done.8, bf16[256,256]{1,0:T(8,128)(2,1)} %get-tuple-element.19, f32[256]{0:T(256)S(1)} %mul.299, f32[256,1024]{1,0:T(8,128)S(1)} %fusion.37), kind=kOutput, calls=%fused_computation.4 | convolution fusion | flops 136839168 | bytes 1836032 | tf_op jit(solution)/shard_map/dot_general | solution.py:532
  33.9 0.2 fusion.42
  34.1 0.7 fusion.34.therm_ref
  34.9 0.4 fusion.15
  35.3 0.5 copy-done.6
  35.7 0.9 %fusion.26.force_ref = f32[128,256]{1,0:T(8,128)} fusion(bf16[256,128]{1,0:T(8,128)(2,1)S(1)} %copy-done.6, bf16[32,8,256]{2,1,0:T(8,128)(2,1)S(1)} %fusion.15), kind=kOutput, calls=%fused_computation.61 | convolution fusion | flops 16777216 | bytes 327680 | tf_op jit(solution)/shard_map/dot_general | solution.py:600
  36.6 28.8 %reduce_gradients.1 = (bf16[4608,128]{1,0:T(8,128)(2,1)}, f32[8,2,128]{2,1,0:T(2,128)}) custom-call(f32[256,1024]{1,0:T(8,128)} %fusion.36.up_ref, f32[1024,256]{1,0:T(8,128)} %fusion.28.down_ref, f32[128,256]{1,0:T(8,128)} %fusion.26.force_ref, f32[1,256]{1,0:T(1,128)} %bitcast.103, f32[1,256]{1,0:T(1,128)} %bitcast.102, f32[1,256]{1,0:T(1,128)} %bitcast.101, ...), custom_call_target="tpu_custom_call" | custom-call | tf_op jit(solution)/shard_map/reduce_gradients/pallas_call | solution.py:285
  65.4 3.0 %unpack_gradients.1 = (bf16[256,1024]{1,0:T(8,128)(2,1)}, bf16[1024,256]{1,0:T(8,128)(2,1)}, bf16[128,256]{1,0:T(8,128)(2,1)}, bf16[9,256]{1,0:T(8,128)(2,1)}, b...) custom-call(bf16[4608,128]{1,0:T(8,128)(2,1)} %get-tuple-element.22.whole, f32[8,2,128]{2,1,0:T(2,128)} %get-tuple-element.23.therm), custom_call_target="tpu_custom_call" | custom-call | tf_op jit(solution)/shard_map/unpack_gradients/pallas_call | solution.py:310
  (39 shorter events, 1.2 us)
Async XLA Ops:
  0.6 21.1 %copy-start = (bf16[256,1024]{1,0:T(8,128)(2,1)S(1)}, bf16[256,1024]{1,0:T(8,128)(2,1)}, u32[]{:S(2)}) copy-start(bf16[256,1024]{1,0:T(8,128)(2,1)} %param.19) | copy-start | bytes 1572868
  18.4 3.4 %copy-start.7 = (f32[256]{0:T(256)S(1)}, f32[256]{0:T(256)}, u32[]{:S(2)}) copy-start(f32[256]{0:T(256)} %param.18) | copy-start | bytes 3076
  21.3 0.9 %copy-start.4 = (bf16[1,32,8,256]{3,2,1,0:T(8,128)(2,1)S(1)}, bf16[1,32,8,256]{3,2,1,0:T(8,128)(2,1)}, u32[]{:S(2)}) copy-start(bf16[1,32,8,256]{3,2,1,0:T(8,128)(2,1)} %param.25) | copy-start | bytes 393220
  21.3 1.1 %copy-start.8 = (bf16[1024,256]{1,0:T(8,128)(2,1)S(1)}, bf16[1024,256]{1,0:T(8,128)(2,1)}, u32[]{:S(2)}) copy-start(bf16[1024,256]{1,0:T(8,128)(2,1)} %param.20) | copy-start | bytes 1572868
  23.3 1.2 %copy-start.1 = (f32[34,10,256]{2,1,0:T(8,128)S(1)}, f32[34,10,256]{2,1,0:T(8,128)}, u32[]{:S(2)}) copy-start(f32[34,10,256]{2,1,0:T(8,128)} %get-tuple-element.20) | copy-start | bytes 1044484
  25.5 9.3 %collective-permute-start = (f32[32,1,256]{2,1,0:T(1,128)S(1)}, f32[32,1,256]{2,1,0:T(1,128)S(1)}, u32[]{:S(2)}, u32[]{:S(2)}) collective-permute-start(f32[32,1,256]{2,1,0:T(1,128)S(1)} %get-tuple-element.46), channel_id=1, source_target_pairs={{0,1},{1,2},{2,3},{3,4},{4,5},{5,6},{6,7},{7,0},{8,9},{9,10},{10,1... | collective-permute-start | bytes 98312 | tf_op jit(solution)/shard_map/ppermute | solution.py:480
  25.6 9.2 %collective-permute-start.1 = (f32[32,1,256]{2,1,0:T(1,128)S(1)}, f32[32,1,256]{2,1,0:T(1,128)S(1)}, u32[]{:S(2)}, u32[]{:S(2)}) collective-permute-start(f32[32,1,256]{2,1,0:T(1,128)S(1)} %get-tuple-element.47), channel_id=1, source_target_pairs={{1,0},{2,1},{3,2},{4,3},{5,4},{6,5},{7,6},{0,7},{9,8},{10,9},{11,1... | collective-permute-start | bytes 98312 | tf_op jit(solution)/shard_map/ppermute | solution.py:482
  32.4 1.4 %copy-start.5 = (bf16[256,128]{1,0:T(8,128)(2,1)S(1)}, bf16[256,128]{1,0:T(8,128)(2,1)}, u32[]{:S(2)}) copy-start(bf16[256,128]{1,0:T(8,128)(2,1)} %param.21) | copy-start | bytes 196612
  33.9 1.4 %copy-start.3 = (bf16[256,256]{1,0:T(8,128)(2,1)}, bf16[256,256]{1,0:T(8,128)(2,1)S(1)}, u32[]{:S(2)}) copy-start(bf16[256,256]{1,0:T(8,128)(2,1)S(1)} %fusion.1) | copy-start | bytes 393220
  34.9 0.8 %copy-start.6 = (bf16[256,128]{1,0:T(8,128)(2,1)S(1)}, bf16[256,128]{1,0:T(8,128)(2,1)}, u32[]{:S(2)}) copy-start(bf16[256,128]{1,0:T(8,128)(2,1)} %get-tuple-element.21) | copy-start | bytes 196612
  35.3 30.1 %copy-start.2 = (bf16[32,8,256]{2,1,0:T(8,128)(2,1)}, bf16[32,8,256]{2,1,0:T(8,128)(2,1)S(1)}, u32[]{:S(2)}) copy-start(bf16[32,8,256]{2,1,0:T(8,128)(2,1)S(1)} %fusion.15) | copy-start | bytes 393220
